TPU v7x, 512 devices: a whole 4x4x16 slice. The times are simulated.
512 devices in a mesh: chan: 32 (over x, z_lo), tm: 16 (over y, z_hi, core).
Axes of the slice: x: 4, y: 4, z: 16 (z_hi: 2, z_lo: 8; z = z_hi * 8 + z_lo), core: 2. Of those that a mesh axis runs over, the one named last changes fastest.
Arguments:
- records: bfloat16 [512, 16, 768], P('chan', 'tm'), may hold values from -64 to 64
- source_ids: int32 [2, 128], replicated, may hold values from 0 to 511, as said below
- pair_rows: int32 [2, 16384], P(None, 'chan'), may hold values from 0 to 2047, as said below
- pair_bins: int32 [2, 16384], P(None, 'chan'), may hold values from 0 to 511, as said below
- bin_places: int32 [512], replicated, may hold values from 0 to 511, as said below
Outputs:
- stacks: float32 [512, 1024], P('tm', 'chan')
Inputs may be any that keep to these rules, and one draw needn't show every extreme that they name: `source_ids`: in each step the 128 ids are distinct. `pair_rows`: within each step, the 512 entries of one block of columns are distinct. `pair_bins`: within each step and block of 512 columns, at most 64 entries name bins whose owner bin_places // 32 is the same, and one owner is named by exactly 64. `bin_places`: each bin has its own row: the entries are a permutation.
All inputs are finite; a program needn't handle non-finite values.
Results may differ from a plain program's by a relative error of at most 0.004.
Values may be sent and summed in bfloat16 or wider, within the bound.
No kernel may reach another device: no remote copies, remote signals or barrier semaphores. Data moves between devices by JAX's collectives and lax.ppermute only.
A program may use at most 64 MiB of HBM per device.

v0:
```python
import jax
import jax.numpy as jnp
from jax import lax
from jax.sharding import PartitionSpec as P

LAGS = 1024
BIN_DEV = 32


def normalize(records):
    values = records.astype(jnp.float32)
    mean_square = jnp.mean(values * values, axis=-1, keepdims=True)
    return (values * lax.rsqrt(mean_square + 1e-06)).astype(jnp.bfloat16)


def hankel_blocks(series, left_pad):
    padded = jnp.pad(series, ((0, 0), (0, 0), (left_pad, LAGS - left_pad)))
    block_count = padded.shape[-1] // 128
    blocked = padded.reshape(series.shape[0], series.shape[1], block_count, 128)
    joined = jnp.concatenate([blocked[:, :, :-1], blocked[:, :, 1:]], axis=-1)
    return jnp.stack([joined[..., offset : offset + 128] for offset in range(128)], axis=-2)


def correlate(sources, hankel, chosen):
    src_count, win_count, sample_count = sources.shape
    time_blocks = sample_count // 128
    emitters = sources.reshape(src_count, win_count, time_blocks, 128)

    def lag_block(lag_start):
        part_blocks = lax.dynamic_slice_in_dim(hankel, lag_start, time_blocks, axis=2)
        full_rows = jnp.einsum(
            "swki,rwkij->rsj", emitters, part_blocks, preferred_element_type=jnp.float32
        )
        return jnp.take(full_rows.reshape(-1, 128), chosen, axis=0)

    stacked = lax.map(lag_block, jnp.arange(LAGS // 128))
    ordered = jnp.transpose(stacked, (1, 0, 2)).reshape(chosen.shape[0], LAGS)
    return jnp.flip(ordered, axis=1)


def shards(records, source_ids, pair_rows, pair_bins, bin_places):
    channel_count = records.shape[0]
    sample_count = records.shape[2]
    step_count = source_ids.shape[0]
    pair_count = pair_rows.shape[1]
    bin_count = bin_places.shape[0]
    tm_count = lax.axis_size("tm")
    capacity = 2 * pair_count // tm_count
    normed = normalize(records)
    hankel = hankel_blocks(normed, LAGS - 1 - LAGS // 2)
    global_ids = lax.axis_index("chan") * channel_count + jnp.arange(channel_count)
    picker = (source_ids[:, :, None] == global_ids[None, None, :]).astype(jnp.bfloat16)
    totals = jnp.zeros((BIN_DEV, LAGS), jnp.float32)
    bin_range = jnp.arange(bin_count)
    for step_index in range(step_count):
        offered_step = jnp.einsum(
            "sc,cwt->swt", picker[step_index], normed, preferred_element_type=jnp.float32
        )
        sources = lax.psum(offered_step.astype(jnp.bfloat16), "chan")
        chosen_rows = correlate(sources, hankel, pair_rows[step_index])
        matches = pair_bins[step_index][:, None] == bin_range[None, :]
        placed = jnp.sum(jnp.where(matches, bin_places[None, :], 0), axis=1)
        owner_of = placed // BIN_DEV
        member = (owner_of[:, None] == jnp.arange(tm_count)[None, :]).astype(jnp.int32)
        earlier = jnp.sum((jnp.cumsum(member, axis=0) - member) * member, axis=1)
        target = owner_of * capacity + earlier
        outgoing = jnp.zeros((tm_count * capacity, LAGS), jnp.float32).at[target].set(chosen_rows)
        labels = jnp.full((tm_count * capacity,), -1, jnp.int32).at[target].set(placed % BIN_DEV)
        arrived, arrived_labels = (
            lax.all_to_all(outgoing, "tm", split_axis=0, concat_axis=0, tiled=True),
            lax.all_to_all(labels, "tm", split_axis=0, concat_axis=0, tiled=True),
        )
        selector = (jnp.arange(BIN_DEV)[:, None] == arrived_labels[None, :]).astype(jnp.float32)
        totals = totals + jnp.dot(
            selector, arrived, precision=lax.Precision.HIGHEST, preferred_element_type=jnp.float32
        )
    shares = lax.psum_scatter(totals, "chan", scatter_dimension=1, tiled=True)
    return shares / sample_count


def solution(mesh):
    in_specs = (P("chan", "tm", None), P(), P(None, "chan"), P(None, "chan"), P())
    out_specs = P("tm", "chan")
    return jax.shard_map(shards, mesh=mesh, in_specs=in_specs, out_specs=out_specs, check_vma=False)
```

profile of v0, /device:TPU:24, one launch (start us, length us, event | category | flops | bytes accessed | tf_op | source)
XLA Modules:
  0.0 1212.5 jit_solution(5245608293458728651)
XLA Ops:
  7.3 1.1 select_reduce_fusion
  8.5 1.2 reduce-window.14
  10.0 2.4 scatter_custom_fusion
  13.1 18.0 %all-to-all-start = ((s32[16,64,1]{1,2,0:T(1,128)}), s32[16,64,1]{1,2,0:T(1,128)S(1)}, u32[]{:S(2)}, u32[]{:S(2)}) async-start(s32[16,64,1]{1,2,0:T(1,128)} %bitcast.24), calls=%async_computation | async-start | bytes 16384 | tf_op jit(solution)/shard_map/all_to_all | solution.py:71
  31.2 0.9 fusion.270
  32.0 0.8 fusion.271
  34.0 0.8 copy.181
  34.8 0.8 copy.188
  127.1 1.1 reduce-window.16
  130.1 10.9 copy.182
  141.0 2.4 scatter_custom_fusion.2
  144.1 332.6 %all-reduce.4.cloned.1.call-done = (bf16[128,1,6,128]{0,3,2,1:T(8,128)(2,1)}, bf16[128,1,6,128]{0,3,2,1:T(8,128)(2,1)}) async-done(((bf16[128,1,6,128]{0,3,2,1:T(8,128)(2,1)}, bf16[128,1,6,128]{0,3,2,1:T(8,128)(2,1)}), (bf16[128,1,6,128]{0,3,2,1:T(8,128)(2,1)}, bf16[128,1,6,128]{0,3,2,1:T(8,128)(2,1)})) %all-reduce.4.cloned.1.call-update) | async-done | bytes 393232 | tf_op jit(solution)/shard_map/psum | solution.py:59
  476.7 1.7 copy.183
  478.4 15.2 %all-to-all-start.2 = ((s32[16,64,1]{1,2,0:T(1,128)}), s32[16,64,1]{1,2,0:T(1,128)S(1)}, u32[]{:S(2)}, u32[]{:S(2)}) async-start(s32[16,64,1]{1,2,0:T(1,128)} %bitcast.167), calls=%async_computation.2 | async-start | bytes 16384 | tf_op jit(solution)/shard_map/all_to_all | solution.py:71
  493.9 52.3 %while.20 = (s32[]{:T(128)}, f32[8,512,128]{1,2,0:T(8,128)S(1)}, s32[8]{0:T(128)S(1)}, bf16[16,1,13,128,128]{4,3,2,0,1:T(8,128)(2,1)}, bf16[128,1,6,128]{3,0,2,1...) while((s32[]{:T(128)}, f32[8,512,128]{1,2,0:T(8,128)S(1)}, s32[8]{0:T(128)S(1)}, ...), condition=%wide.region_8.10_spmd, body=%wide.region_7.9_spmd.sunk | while | flops 402724352 | bytes 6503571 | solution.py:36
  496.5 2.6 fusion.307
  499.1 1.0 gather_fusion
  503.0 2.6 fusion.307
  505.6 1.0 gather_fusion
  509.5 2.6 fusion.307
  512.2 1.0 gather_fusion
  516.1 2.6 fusion.307
  518.7 1.0 gather_fusion
  522.6 2.6 fusion.307
  525.2 1.0 gather_fusion
  529.2 2.6 fusion.307
  531.8 1.0 gather_fusion
  535.7 2.6 fusion.307
  538.3 1.0 gather_fusion
  542.2 2.6 fusion.307
  544.9 1.0 gather_fusion
  546.2 10.5 rev.7
  556.8 2.0 copy.185
  558.7 4.4 scatter_custom_fusion.1
  563.2 14.4 %all-to-all-start.1 = ((f32[16,64,1024]{2,1,0:T(8,128)}), f32[16,64,1024]{2,1,0:T(8,128)}, u32[]{:S(2)}, u32[]{:S(2)}) async-start(f32[16,64,1024]{2,1,0:T(8,128)} %bitcast.677), calls=%async_computation.1 | async-start | bytes 8388608 | tf_op jit(solution)/shard_map/all_to_all | solution.py:70
  577.6 0.8 copy.190
  578.7 51.7 %while.21 = (s32[]{:T(128)}, f32[8,512,128]{1,2,0:T(8,128)S(1)}, s32[8]{0:T(128)S(1)}, bf16[16,1,13,128,128]{4,3,2,0,1:T(8,128)(2,1)}, bf16[128,1,6,128]{3,0,2,1...) while((s32[]{:T(128)}, f32[8,512,128]{1,2,0:T(8,128)S(1)}, s32[8]{0:T(128)S(1)}, ...), condition=%wide.region_17.19_spmd, body=%wide.region_16.18_spmd.sunk | while | flops 402724352 | bytes 6503571 | solution.py:36
  581.2 2.6 fusion.310
  583.8 1.0 gather_fusion.1
  587.6 2.6 fusion.310
  590.2 1.0 gather_fusion.1
  594.1 2.6 fusion.310
  596.7 1.0 gather_fusion.1
  600.5 2.6 fusion.310
  603.2 1.0 gather_fusion.1
  607.0 2.6 fusion.310
  609.6 1.0 gather_fusion.1
  613.5 2.6 fusion.310
  616.1 1.0 gather_fusion.1
  619.9 2.6 fusion.310
  622.5 1.0 gather_fusion.1
  626.4 2.6 fusion.310
  629.0 1.0 gather_fusion.1
  630.4 10.5 rev.8
  640.8 1.9 copy.192
  642.8 4.4 scatter_custom_fusion.3
  647.2 31.9 %all-to-all-done.1 = f32[16,64,1024]{2,1,0:T(8,128)} async-done(((f32[16,64,1024]{2,1,0:T(8,128)}), f32[16,64,1024]{2,1,0:T(8,128)}, u32[]{:S(2)}, u32[]{:S(2)}) %all-to-all-start.1) | async-done | bytes 4194336 | tf_op jit(solution)/shard_map/all_to_all | solution.py:70
  679.1 16.4 %all-to-all-start.3 = ((f32[16,64,1024]{2,1,0:T(8,128)}), f32[16,64,1024]{2,1,0:T(8,128)}, u32[]{:S(2)}, u32[]{:S(2)}) async-start(f32[16,64,1024]{2,1,0:T(8,128)} %bitcast.678), calls=%async_computation.3 | async-start | bytes 8388608 | tf_op jit(solution)/shard_map/all_to_all | solution.py:70
  697.5 3.8 fusion.14
  701.4 108.3 %all-to-all-done.3 = f32[16,64,1024]{2,1,0:T(8,128)} async-done(((f32[16,64,1024]{2,1,0:T(8,128)}), f32[16,64,1024]{2,1,0:T(8,128)}, u32[]{:S(2)}, u32[]{:S(2)}) %all-to-all-start.3) | async-done | bytes 4194336 | tf_op jit(solution)/shard_map/all_to_all | solution.py:70
  809.7 3.8 convolution_add_fusion
  813.5 1.0 copy.196
  814.5 389.8 %reduce-scatter.4.cloned.1.call-done = f32[32,32]{1,0:T(8,128)} async-done(((f32[1024,32]{1,0:T(8,128)}), f32[32,32]{1,0:T(8,128)}) %reduce-scatter.4.cloned.1.call-update) | async-done | bytes 4112
  1204.3 0.8 copy.197
  (286 shorter events, 114.6 us)
Async XLA Ops:
  13.1 465.3 %all-to-all-start = ((s32[16,64,1]{1,2,0:T(1,128)}), s32[16,64,1]{1,2,0:T(1,128)S(1)}, u32[]{:S(2)}, u32[]{:S(2)}) async-start(s32[16,64,1]{1,2,0:T(1,128)} %bitcast.24), calls=%async_computation | async-start | bytes 16384 | tf_op jit(solution)/shard_map/all_to_all | solution.py:71
  31.1 445.6 %all-reduce.4.cloned.1.call-start = ((), (), s32[]{:S(2)}) async-start(), calls=%async_computation.6 | async-start | bytes 786432 | tf_op jit(solution)/shard_map/psum | solution.py:59
  67.0 62.4 %copy-start.1 = (s32[2,512]{1,0:T(2,128)S(1)}, s32[2,512]{1,0:T(2,128)}, u32[]{:S(2)}) copy-start(s32[2,512]{1,0:T(2,128)} %param.13) | copy-start | bytes 12292
  478.4 84.7 %all-to-all-start.2 = ((s32[16,64,1]{1,2,0:T(1,128)}), s32[16,64,1]{1,2,0:T(1,128)S(1)}, u32[]{:S(2)}, u32[]{:S(2)}) async-start(s32[16,64,1]{1,2,0:T(1,128)} %bitcast.167), calls=%async_computation.2 | async-start | bytes 16384 | tf_op jit(solution)/shard_map/all_to_all | solution.py:71
  556.8 20.9 %copy-start = (bf16[128,1,6,128]{0,3,2,1:T(8,128)(2,1)S(1)}, bf16[128,1,6,128]{0,3,2,1:T(8,128)(2,1)}, u32[]{:S(2)}) copy-start(bf16[128,1,6,128]{0,3,2,1:T(8,128)(2,1)} %get-tuple-element.147) | copy-start | bytes 589828
  563.2 115.9 %all-to-all-start.1 = ((f32[16,64,1024]{2,1,0:T(8,128)}), f32[16,64,1024]{2,1,0:T(8,128)}, u32[]{:S(2)}, u32[]{:S(2)}) async-start(f32[16,64,1024]{2,1,0:T(8,128)} %bitcast.677), calls=%async_computation.1 | async-start | bytes 8388608 | tf_op jit(solution)/shard_map/all_to_all | solution.py:70
  679.1 130.6 %all-to-all-start.3 = ((f32[16,64,1024]{2,1,0:T(8,128)}), f32[16,64,1024]{2,1,0:T(8,128)}, u32[]{:S(2)}, u32[]{:S(2)}) async-start(f32[16,64,1024]{2,1,0:T(8,128)} %bitcast.678), calls=%async_computation.3 | async-start | bytes 8388608 | tf_op jit(solution)/shard_map/all_to_all | solution.py:70
  695.5 508.8 %reduce-scatter.4.cloned.1.call-start = ((), (), s32[]{:S(2)}) async-start(), calls=%async_computation.5 | async-start | bytes 540672
Sparse Core Ops, SparseCore 0:
  35.8 440.8 all-reduce.3
  814.7 389.5 reduce-scatter.3
where the time goes:
time: 1210 us
  waiting for transfers between devices  863 us (71%)
  other arithmetic  103 us (9%)
  local copies, waits for them, and re-layouts  88.7 us (7%)
  starting transfers between devices  64.1 us (5%)
  matrix products  49.5 us (4%)
  loops' own time  31.4 us (3%)
  between operations  13.7 us (1%)
    unnamed x3, waiting for transfers between devices  390 us
    psum x1, waiting for transfers between devices, shards(): sources = lax.psum(offered_step.astype(jnp.bfloat16), 'chan')  333 us
    all_to_all x2, waiting for transfers between devices, shards(): lax.all_to_all(outgoing, 'tm', split_axis=0, concat_axis=0, tiled=True)  140 us
    unnamed x126, other arithmetic  91.3 us
    dot_general x16, matrix products, lag_block(): jnp.einsum('swki,rwkij->rsj', emitters, part_blocks, preferred_element_ty...  41.5 us
    all_to_all x2, starting transfers between devices, shards(): lax.all_to_all(labels, 'tm', split_axis=0, concat_axis=0, tiled=True)  33.2 us
    another operation x2, loops' own time, correlate(): stacked = lax.map(lag_block, jnp.arange(LAGS // 128))  31.4 us
    all_to_all x2, starting transfers between devices, shards(): lax.all_to_all(outgoing, 'tm', split_axis=0, concat_axis=0, tiled=True)  30.8 us
  transfers between devices with their start and end apart: 6, of which 4 were waited for; matrix products, arithmetic and copies ran while one was open for 19% of the time, Pallas kernels for 0%

commit v1 on v0

v1 whole, which is shorter than its diff:
```python
import functools

import jax
import jax.numpy as jnp
import numpy as np
from jax import lax
from jax.experimental import pallas as pl
from jax.experimental.pallas import tpu as pltpu
from jax.sharding import Mesh, PartitionSpec as P

NT = 768
LAGS = 1024
SRC = 128
CH_DEV = 16
CHANNELS = 512
BIN_DEV = 32
BINS = 512
PAIRS = 1024
NFFT = 2048
PARTS = 8
SLOTS = NFFT // 4 // PARTS
LANES = 128
WIDE = 2 * LANES

bf16 = jnp.bfloat16
f32 = jnp.float32
dot = functools.partial(jnp.dot, preferred_element_type=f32)
HBM = pl.BlockSpec(memory_space=pltpu.MemorySpace.HBM)
VMEM = pl.BlockSpec(memory_space=pltpu.VMEM)
SMEM = pl.BlockSpec(memory_space=pltpu.SMEM)


def angles(left, right):
    return (np.outer(left, right) % (2 * NFFT)) * (np.pi / NFFT)


def forward_table():
    phase = angles(np.arange(NT), 2 * np.arange(NFFT // 4) + 1)
    return np.concatenate([np.cos(phase), np.sin(phase)], axis=1).astype(bf16)


def inverse_tables():
    lag = np.arange(LAGS) - LAGS // 2
    phase = angles(2 * np.arange(SLOTS) + 1, lag)
    turn = angles(np.arange(PARTS) * 2 * SLOTS, lag)
    scale = 2.0 / (NFFT * NT)
    sign = 1 - 2 * (lag % 2)
    cos, sin = np.cos(phase), np.sin(phase)
    base = np.concatenate([cos, sign * cos, sin, sign * sin], axis=0).astype(bf16)
    turns = scale * np.stack([np.cos(turn), np.sin(turn)], axis=1)
    return base, turns.astype(np.float32)


def spectra_kernel(records_hbm, table_hbm, rows_hbm, bins_hbm, places_hbm, out_ref, *scratch):
    *refs, sems = scratch
    sources = (rows_hbm, bins_hbm, places_hbm, records_hbm, table_hbm)
    copies = [pltpu.make_async_copy(s, d, sems.at[i]) for i, (s, d) in enumerate(zip(sources, refs))]
    for copy in copies:
        copy.start()
    rows_ref, bins_ref, places_ref, records_ref, table_ref = refs
    for copy in copies[:3]:
        copy.wait()

    place = places_ref[...]
    owner, slot = place // BIN_DEV, place % BIN_DEV
    order = (slot // 8) * 128 + (owner // 4) * 32 + (owner % 2) * 16
    order = order + (slot % 4) * 4 + ((owner // 2) % 2) * 2 + (slot // 4) % 2
    digits = jnp.broadcast_to(order - BINS // 2, (8, BINS)).astype(f32).astype(bf16)
    bins = jnp.concatenate([bins_ref[0:1, :], bins_ref[1:2, :]], axis=1)
    match = lax.broadcasted_iota(jnp.int32, (BINS, PAIRS), 0) == bins
    spots = dot(digits, match.astype(f32).astype(bf16))[0:1]
    rows = jnp.concatenate([rows_ref[0:1, :], rows_ref[1:2, :]], axis=1)
    lists = [(rows // SRC).astype(f32), (rows % SRC).astype(f32), spots, spots]
    packed = [item[:, 256 * j : 256 * (j + 1)] for item in lists for j in range(4)]
    packed = jnp.concatenate(packed, axis=0).astype(bf16)

    copies[3].wait()
    values = records_ref[...].astype(f32)
    mean_square = jnp.mean(values * values, axis=-1, keepdims=True)
    normed = values * lax.rsqrt(mean_square + 1e-06)
    odd = lax.broadcasted_iota(jnp.int32, normed.shape, 1) % 2 == 1
    split = jnp.concatenate([jnp.where(odd, 0.0, normed), jnp.where(odd, normed, 0.0)], axis=0).astype(bf16)
    copies[4].wait()
    sums = dot(split, table_ref[...])
    even, odd = sums[:CH_DEV], sums[CH_DEV:]
    lower, upper = even + odd, even - odd
    half = PARTS * SLOTS
    for z in range(PARTS):
        cuts = [slice(start + SLOTS * z, start + SLOTS * (z + 1)) for start in (0, half)]
        part = jnp.concatenate([piece[:, cut] for cut in cuts for piece in (lower, upper)], axis=1)
        out_ref[z, :CH_DEV, :] = part.astype(bf16)
        out_ref[z, CH_DEV:, :] = packed


def make_spectra(records, rows, bins, places):
    table = jnp.asarray(forward_table())
    inputs = (rows, bins, places, records, table)
    return pl.pallas_call(
        spectra_kernel,
        out_shape=jax.ShapeDtypeStruct((PARTS, 2 * CH_DEV, WIDE), bf16),
        in_specs=[HBM] * 5,
        out_specs=VMEM,
        scratch_shapes=[pltpu.VMEM(item.shape, item.dtype) for item in inputs] + [pltpu.SemaphoreType.DMA((5,))],
        name="spectra",
    )(records, table, rows, bins, places)


def pairs_kernel(own_ref, all_ref, ids_ref, out_ref, src_ref, recv_ref, total_ref):
    ids = jnp.concatenate([ids_ref[...].astype(f32)] + [jnp.zeros((6, SRC), f32)], axis=0).T
    lane = lax.broadcasted_iota(jnp.int32, (SRC, CHANNELS), 1).astype(f32)
    for k in range(2):
        pick = (ids[:, k : k + 1] == lane).astype(f32).astype(bf16)
        src_ref[k] = dot(pick, all_ref[...]).astype(bf16)
    for z in range(PARTS):
        recv_ref[CH_DEV * z : CH_DEV * (z + 1), :] = own_ref[z, :CH_DEV, :]
    lane = lax.broadcasted_iota(jnp.int32, (256, SRC), 1).astype(f32)
    bin_row = (lax.broadcasted_iota(jnp.int32, (BINS, 256), 0) - BINS // 2).astype(f32).astype(bf16)
    one, zero = jnp.ones((BINS, 256), bf16), jnp.zeros((BINS, 256), bf16)
    for z in range(PARTS):
        lists = own_ref[z, CH_DEV:, :]
        columns = lists.astype(f32).T
        products, matches = [], []
        for j in range(4):
            pick_r = (columns[:, j : j + 1] + float(z * CH_DEV) == lane).astype(f32).astype(bf16)
            pick_s = (columns[:, 4 + j : 5 + j] == lane).astype(f32).astype(bf16)
            r, s = dot(pick_r, recv_ref[...]), dot(pick_s, src_ref[j // 2])
            rc, rs, sc, ss = r[:, :LANES], r[:, LANES:], s[:, :LANES], s[:, LANES:]
            product = jnp.concatenate([rc * sc + rs * ss, rs * sc - rc * ss], axis=1)
            products.append(product.astype(bf16))
            matches.append(jnp.where(bin_row == lists[8 + j : 9 + j, :], one, zero))
        part = dot(jnp.concatenate(matches, axis=1), jnp.concatenate(products, axis=0))
        if z == 0:
            total_ref[...] = part
        elif z < PARTS - 1:
            total_ref[...] += part
        else:
            out_ref[...] = (total_ref[...] + part).astype(bf16)


def bin_pairs(own, everyone, ids):
    return pl.pallas_call(
        pairs_kernel,
        out_shape=jax.ShapeDtypeStruct((BINS, WIDE), bf16),
        in_specs=[VMEM, VMEM, VMEM],
        out_specs=VMEM,
        scratch_shapes=[
            pltpu.VMEM((2, SRC, WIDE), bf16),
            pltpu.VMEM((PARTS * CH_DEV, WIDE), bf16),
            pltpu.VMEM((BINS, WIDE), f32),
        ],
        compiler_params=pltpu.CompilerParams(vmem_limit_bytes=32 << 20),
        name="bin_pairs",
    )(own, everyone, ids)


def inverse_kernel(part_ref, parts_ref, base_ref, turns_ref, out_ref):
    spectrum = jnp.sum(parts_ref[...].astype(f32), axis=0)
    high = spectrum.astype(bf16)
    low = (spectrum - high.astype(f32)).astype(bf16)
    both = jnp.concatenate([high, low], axis=0)
    re, im = both[:, :LANES], both[:, LANES:]
    cos, sin = base_ref[:LANES, :], base_ref[LANES:, :]
    real = dot(re, cos) - dot(im, sin)
    imag = dot(re, sin) + dot(im, cos)
    turns = turns_ref[part_ref[0]]
    lags = (real[:16] + real[16:]) * turns[0:1] - (imag[:16] + imag[16:]) * turns[1:2]
    for group in range(8):
        tile = lags[:, 128 * group : 128 * (group + 1)]
        for quarter in range(4):
            lane = slice(32 * quarter, 32 * (quarter + 1))
            out_ref[4 * group + quarter] = jnp.concatenate([tile[4 * c : 4 * c + 4, lane] for c in range(4)], axis=1)


def invert(parts):
    base, turns = inverse_tables()
    part = lax.axis_index("zl").astype(jnp.int32).reshape(1)
    return pl.pallas_call(
        inverse_kernel,
        out_shape=jax.ShapeDtypeStruct((32, 4, 128), f32),
        in_specs=[SMEM, VMEM, VMEM, VMEM],
        out_specs=VMEM,
        compiler_params=pltpu.CompilerParams(vmem_limit_bytes=32 << 20),
        name="invert",
    )(part, parts, jnp.asarray(base), jnp.asarray(turns))


def exchange(value, axes):
    return lax.all_to_all(value, axes, split_axis=0, concat_axis=0, tiled=True)


def shards(records, source_ids, pair_rows, pair_bins, bin_places):
    spectra = make_spectra(records.reshape(CH_DEV, NT), pair_rows, pair_bins, bin_places.reshape(1, BINS))
    own = exchange(spectra, "zl")
    offered = own[:, :CH_DEV, :].reshape(1, SRC, WIDE)
    everyone = exchange(jnp.broadcast_to(offered, (4, SRC, WIDE)), "x").reshape(CHANNELS, WIDE)
    binned = bin_pairs(own, everyone, source_ids)
    parts = exchange(binned.reshape(32, 16, WIDE), ("x", "y", "core"))
    shares = exchange(invert(parts).reshape(64, 2, 128), ("x", "zl", "zh"))
    return jnp.sum(shares.reshape(4, 16, 2, 128), axis=1).reshape(BIN_DEV, 32)


def solution(mesh):
    fine = Mesh(mesh.devices.reshape(4, 8, 4, 2, 2), ("x", "zl", "y", "zh", "core"))
    chan, tm = ("x", "zl"), ("y", "zh", "core")
    in_specs = (P(chan, tm, None), P(), P(None, chan), P(None, chan), P())
    return jax.shard_map(shards, mesh=fine, in_specs=in_specs, out_specs=P(tm, chan), check_vma=False)
```

time: 1210 us -> 84.6 us (0.07)
  the two profiles are of different devices: /device:TPU:24 before, /device:TPU:1 now
where the time goes in v1:
time: 84.6 us; the launch traced here: 84.2 us
  blocking collectives  55.9 us (66%)
  Pallas kernels  9.3 us (11%)
  starting transfers between devices  9.21 us (11%)
  waiting for transfers between devices  8.98 us (11%)
    all_to_all x3, blocking collectives, exchange(): return lax.all_to_all(value, axes, split_axis=0, concat_axis=0, tiled=True)  55.9 us
    all_to_all x1, starting transfers between devices, exchange(): return lax.all_to_all(value, axes, split_axis=0, concat_axis=0, tiled=True)  9.21 us
    all_to_all x1, waiting for transfers between devices, exchange(): return lax.all_to_all(value, axes, split_axis=0, concat_axis=0, tiled=True)  8.98 us
    pallas_call x1, Pallas kernels, bin_pairs(): pl.pallas_call(pairs_kernel, out_shape=jax.ShapeDtypeStruct((BINS, WIDE),...  6.21 us
    pallas_call x1, Pallas kernels, make_spectra(): pl.pallas_call(spectra_kernel, out_shape=jax.ShapeDtypeStruct((PARTS, 2 *...  2.64 us
  transfers between devices with their start and end apart: 1, of which 1 were waited for; matrix products, arithmetic and copies ran while one was open for 0% of the time, Pallas kernels for 0%

profile of v1, /device:TPU:1, one launch (start us, length us, event | category | flops | bytes accessed | tf_op | source)
XLA Modules:
  0.0 84.2 jit_solution(1987842745873228126)
XLA Ops:
  0.0 0.0 copy-start.2
  0.0 2.6 %spectra.1 = bf16[8,32,256]{2,1,0:T(8,128)(2,1)} custom-call(bf16[16,768]{1,0:T(8,128)(2,1)} %bitcast.12, bf16[768,1024]{1,0:T(8,128)(2,1)} %constant.14.clone.table_hbm, s32[2,512]{1,0:T(2,128)} %rows_hbm.1, s32[2,512]{1,0:T(2,128)} %bins_hbm.1, s32[1,512]{1,0:T(1,128)} %bitcast.13), custom_call_target="tpu_custom_call" | custom-call | tf_op jit(solution)/shard_map/spectra/pallas_call | solution.py:98
  2.7 0.0 copy-start
  2.7 0.0 copy-start.1
  2.7 23.5 %all_to_all.20.own_ref = bf16[8,32,256]{2,1,0:T(8,128)(2,1)S(1)} all-to-all(bf16[8,32,256]{2,1,0:T(8,128)(2,1)} %spectra.1), channel_id=1, replica_groups=mesh['x'=4,'zl'=8,'y'=4,'zh'=2,'core'=2] {'zl'}, dimensions={0} | all-to-all | bytes 262144 | tf_op jit(solution)/shard_map/all_to_all | solution.py:188
  26.3 9.3 %all_to_all.21 = bf16[4,128,256]{2,1,0:T(8,128)(2,1)S(1)} all-to-all(bf16[4,128,256]{2,1,0:T(8,128)(2,1)S(1)} %broadcast_in_dim.8), channel_id=1, replica_groups=mesh['x'=4,'zl'=8,'y'=4,'zh'=2,'core'=2] {'x'}, dimensions={0} | all-to-all | bytes 524288 | tf_op jit(solution)/shard_map/all_to_all | solution.py:188
  35.6 0.0 copy-done.2
  35.6 6.2 %bin_pairs.1 = bf16[512,256]{1,0:T(8,128)(2,1)} custom-call(bf16[8,32,256]{2,1,0:T(8,128)(2,1)S(1)} %all_to_all.20.own_ref, bf16[512,256]{1,0:T(8,128)(2,1)S(1)} %bitcast.9, s32[2,128]{1,0:T(2,128)S(1)} %copy-done.2), custom_call_target="tpu_custom_call" | custom-call | tf_op jit(solution)/shard_map/bin_pairs/pallas_call | solution.py:141
  41.8 9.2 %all-to-all-start.2 = ((bf16[32,16,256]{2,1,0:T(8,128)(2,1)}), bf16[32,16,256]{2,1,0:T(8,128)(2,1)S(1)}, u32[]{:S(2)}, u32[]{:S(2)}) async-start(bf16[32,16,256]{2,1,0:T(8,128)(2,1)} %bitcast.5), calls=%async_computation.2 | async-start | bytes 524288 | tf_op jit(solution)/shard_map/all_to_all | solution.py:188
  51.0 9.0 %all-to-all-done.2.parts_ref = bf16[32,16,256]{2,1,0:T(8,128)(2,1)S(1)} async-done(((bf16[32,16,256]{2,1,0:T(8,128)(2,1)}), bf16[32,16,256]{2,1,0:T(8,128)(2,1)S(1)}, u32[]{:S(2)}, u32[]{:S(2)}) %all-to-all-start.2) | async-done | bytes 262176 | tf_op jit(solution)/shard_map/all_to_all | solution.py:188
  60.0 0.0 copy-done
  60.0 0.0 copy-done.1
  60.0 0.5 invert.1
  60.5 23.0 %all_to_all.22 = f32[64,2,128]{2,1,0:T(2,128)S(1)} all-to-all(f32[64,2,128]{2,1,0:T(2,128)S(1)} %bitcast.10), channel_id=1, replica_groups=mesh['x'=4,'zl'=8,'y'=4,'zh'=2,'core'=2] {'x','zl','zh'}, dimensions={0} | all-to-all | bytes 131072 | tf_op jit(solution)/shard_map/all_to_all | solution.py:188
  83.5 0.7 reshape.33
  (3 shorter events, 0.0 us)
Async XLA Ops:
  0.0 35.6 %copy-start.2 = (s32[2,128]{1,0:T(2,128)S(1)}, s32[2,128]{1,0:T(2,128)}, u32[]{:S(2)}) copy-start(s32[2,128]{1,0:T(2,128)} %ids_ref.1) | copy-start | bytes 3076
  2.7 57.4 %copy-start = (bf16[256,1024]{1,0:T(8,128)(2,1)S(1)}, bf16[256,1024]{1,0:T(8,128)(2,1)}, u32[]{:S(2)}) copy-start(bf16[256,1024]{1,0:T(8,128)(2,1)} %constant.15.clone.base_ref) | copy-start | bytes 1572868
  2.7 57.3 %copy-start.1 = (f32[8,2,1024]{2,1,0:T(2,128)S(1)}, f32[8,2,1024]{2,1,0:T(2,128)}, u32[]{:S(2)}) copy-start(f32[8,2,1024]{2,1,0:T(2,128)} %constant.16.clone.turns_ref) | copy-start | bytes 196612
  41.8 18.2 %all-to-all-start.2 = ((bf16[32,16,256]{2,1,0:T(8,128)(2,1)}), bf16[32,16,256]{2,1,0:T(8,128)(2,1)S(1)}, u32[]{:S(2)}, u32[]{:S(2)}) async-start(bf16[32,16,256]{2,1,0:T(8,128)(2,1)} %bitcast.5), calls=%async_computation.2 | async-start | bytes 524288 | tf_op jit(solution)/shard_map/all_to_all | solution.py:188

commit v2 on v1

v2 whole, which is shorter than its diff:
```python
import functools

import jax
import jax.numpy as jnp
import numpy as np
from jax import lax
from jax.experimental import pallas as pl
from jax.experimental.pallas import tpu as pltpu
from jax.sharding import Mesh, PartitionSpec as P

NT = 768
LAGS = 1024
SRC = 128
CH_DEV = 16
CHANNELS = 512
BIN_DEV = 32
BINS = 512
PAIRS = 1024
NFFT = 1536
PARTS = 8
SLOTS = NFFT // 8 // PARTS
USED = 4 * SLOTS
CUTS = 4
LANES = 128
WIDE = 2 * LANES

bf16 = jnp.bfloat16
f32 = jnp.float32
dot = functools.partial(jnp.dot, preferred_element_type=f32)
HBM = pl.BlockSpec(memory_space=pltpu.MemorySpace.HBM)
VMEM = pl.BlockSpec(memory_space=pltpu.VMEM)
SMEM = pl.BlockSpec(memory_space=pltpu.SMEM)


def iota(shape, axis):
    return lax.broadcasted_iota(jnp.int32, shape, axis)


def angles(left, right):
    return (np.outer(left, right) % (2 * NFFT)) * (np.pi / NFFT)


def two_parts(exact):
    high = exact.astype(bf16)
    return np.stack([high, (exact - high.astype(np.float64)).astype(bf16)])


def forward_table():
    phase = angles(np.arange(NT), 2 * np.arange(NFFT // 8) + 1)
    return two_parts(np.concatenate([np.cos(phase), np.sin(phase)], axis=1))


def inverse_tables():
    lag = np.arange(LAGS) - LAGS // 2
    phase = angles(2 * np.arange(SLOTS) + 1, lag)
    turn = angles(np.arange(PARTS) * 2 * SLOTS, lag)
    scale = 2.0 / (NFFT * NT)
    turns = scale * np.stack([np.cos(turn), np.sin(turn)], axis=1)
    return two_parts(np.concatenate([np.cos(phase), np.sin(phase)], axis=0)), turns.astype(np.float32)


def spectra_kernel(records_hbm, table_hbm, rows_hbm, bins_hbm, places_hbm, out_ref, *scratch):
    *refs, sems = scratch
    rows_ref, bins_ref, places_ref, records_ref, table_ref = refs
    ends = [(rows_hbm, rows_ref), (bins_hbm, bins_ref), (places_hbm, places_ref), (records_hbm, records_ref)]
    for i in range(CUTS):
        cut = pl.ds(i * NT // CUTS, NT // CUTS)
        ends.append((table_hbm.at[:, cut, :], table_ref.at[:, cut, :]))
    copies = [pltpu.make_async_copy(source, target, sems.at[i]) for i, (source, target) in enumerate(ends)]
    for copy in copies:
        copy.start()
    for copy in copies[:3]:
        copy.wait()

    place = places_ref[...]
    owner, slot = place // BIN_DEV, place % BIN_DEV
    order = (slot // 8) * 128 + (owner // 4) * 32 + (owner % 2) * 16
    order = order + (slot % 4) * 4 + ((owner // 2) % 2) * 2 + (slot // 4) % 2
    digits = jnp.broadcast_to(order - BINS // 2, (8, BINS)).astype(f32).astype(bf16)
    bins = jnp.concatenate([bins_ref[0:1, :], bins_ref[1:2, :]], axis=1)
    spots = dot(digits, (iota((BINS, PAIRS), 0) == bins).astype(f32).astype(bf16))[0:1]
    rows = jnp.concatenate([rows_ref[0:1, :], rows_ref[1:2, :]], axis=1)

    chosen = iota((PAIRS // 16, PAIRS), 0) == iota((PAIRS // 16, PAIRS), 1) // 16

    def spread(values, first_lane):
        kept = jnp.where(chosen, values, 0.0).astype(bf16)
        lane = (iota((PAIRS, LANES), 0) % 16 + first_lane == iota((PAIRS, LANES), 1)).astype(f32).astype(bf16)
        return dot(kept, lane)

    lists_1 = spread((rows // SRC).astype(f32), USED) + spread((rows % SRC).astype(f32), USED + 16)
    lists_2 = spread(spots, USED)

    copies[3].wait()
    values = records_ref[...].astype(f32)
    mean_square = jnp.mean(values * values, axis=-1, keepdims=True)
    normed = values * lax.rsqrt(mean_square + 1e-06)
    turn = iota(normed.shape, 1) % 4
    split = jnp.concatenate([jnp.where(turn == k, normed, 0.0) for k in range(4)], axis=0).astype(bf16)
    for copy in copies[4:]:
        copy.wait()
    sums = dot(split, table_ref[0]) + dot(split, table_ref[1])
    half = PARTS * SLOTS
    c0, c1, c2, c3 = (sums[CH_DEV * k : CH_DEV * (k + 1), :half] for k in range(4))
    s0, s1, s2, s3 = (sums[CH_DEV * k : CH_DEV * (k + 1), half:] for k in range(4))
    cosines = (c0 + c2 + c1 + c3, c0 + c2 - c1 - c3, c0 - c2 - s1 + s3, c0 - c2 + s1 - s3)
    sines = (s0 + s2 + s1 + s3, s0 + s2 - s1 - s3, s0 - s2 + c1 - c3, s0 - s2 - c1 + c3)
    gap = jnp.zeros((CH_DEV, LANES - USED), f32)
    for z in range(PARTS):
        cut = slice(SLOTS * z, SLOTS * (z + 1))
        parts = [jnp.concatenate([item[:, cut] for item in items] + [gap], axis=1) for items in (cosines, sines)]
        for x in range(4):
            rows_x = slice(CH_DEV * x, CH_DEV * (x + 1))
            full = jnp.concatenate([parts[0] + lists_1[rows_x], parts[1] + lists_2[rows_x]], axis=1)
            out_ref[PARTS * x + z] = full.astype(bf16)


def make_spectra(records, rows, bins, places):
    table = jnp.asarray(forward_table())
    inputs = (rows, bins, places, records, table)
    return pl.pallas_call(
        spectra_kernel,
        out_shape=jax.ShapeDtypeStruct((4 * PARTS, CH_DEV, WIDE), bf16),
        in_specs=[HBM] * 5,
        out_specs=VMEM,
        scratch_shapes=[pltpu.VMEM(item.shape, item.dtype) for item in inputs] + [
            pltpu.SemaphoreType.DMA((4 + CUTS,))
        ],
        name="spectra",
    )(records, table, rows, bins, places)


def pairs_kernel(step_ref, given_ref, ids_ref, out_ref, src_ref, total_ref):
    ids = jnp.broadcast_to(ids_ref[pl.ds(step_ref[0], 1), :].astype(f32), (8, SRC)).T
    pick = (ids[:, 0:1] == iota((SRC, CHANNELS), 1).astype(f32)).astype(f32).astype(bf16)
    used = iota((SRC, WIDE), 1) % LANES < USED
    src_ref[...] = jnp.where(used, dot(pick, given_ref[...]), 0.0).astype(bf16)
    src_lane = iota((256, SRC), 1).astype(f32)
    recv_lane = (iota((256, 256), 1) - iota((256, 256), 0) // CH_DEV * CH_DEV).astype(f32)
    bin_row = (iota((BINS, 256), 0) - BINS // 2).astype(f32).astype(bf16)
    one, zero = jnp.ones((BINS, 256), bf16), jnp.zeros((BINS, 256), bf16)
    for half in range(2):
        block = slice(256 * half, 256 * (half + 1))
        columns = given_ref[block, :LANES].astype(f32)
        spots = given_ref[block, LANES:].astype(f32).T
        for group in range(4):
            products, matches = [], []
            for j in range(4 * group, 4 * group + 4):
                pick_r = (columns[:, USED + j : USED + j + 1] == recv_lane).astype(f32).astype(bf16)
                pick_s = (columns[:, USED + 16 + j : USED + 17 + j] == src_lane).astype(f32).astype(bf16)
                r, s = dot(pick_r, given_ref[block, :]), dot(pick_s, src_ref[...])
                rc, rs, sc, ss = r[:, :LANES], r[:, LANES:], s[:, :LANES], s[:, LANES:]
                product = jnp.concatenate([rc * sc + rs * ss, rs * sc - rc * ss], axis=1)
                products.append(product.astype(bf16))
                matches.append(jnp.where(bin_row == spots[USED + j : USED + j + 1, :].astype(bf16), one, zero))
            part = dot(jnp.concatenate(matches, axis=1), jnp.concatenate(products, axis=0))
            if half == 0 and group == 0:
                total_ref[...] = part
            elif half == 1 and group == 3:
                out_ref[...] = (total_ref[...] + part).astype(bf16)
            else:
                total_ref[...] += part


def bin_pairs(given, ids):
    step = (lax.axis_index("x") // 2).astype(jnp.int32).reshape(1)
    return pl.pallas_call(
        pairs_kernel,
        out_shape=jax.ShapeDtypeStruct((BINS, WIDE), bf16),
        in_specs=[SMEM, VMEM, VMEM],
        out_specs=VMEM,
        scratch_shapes=[pltpu.VMEM((SRC, WIDE), bf16), pltpu.VMEM((BINS, WIDE), f32)],
        compiler_params=pltpu.CompilerParams(vmem_limit_bytes=32 << 20),
        name="bin_pairs",
    )(step, given, ids)


def inverse_kernel(part_ref, parts_ref, base_ref, turns_ref, out_ref):
    spectrum = jnp.sum(parts_ref[...].astype(f32), axis=0)
    high = spectrum.astype(bf16)
    low = (spectrum - high.astype(f32)).astype(bf16)
    both = jnp.concatenate([high, low], axis=0)
    count = high.shape[0]
    turn = iota((1, LAGS), 1) % 4
    sign = (1 - 2 * (turn % 2)).astype(f32)
    even = jnp.where(turn == 0, 1.0, jnp.where(turn == 2, -1.0, 0.0))
    odd = jnp.where(turn == 1, 1.0, jnp.where(turn == 3, -1.0, 0.0))
    gap = jnp.zeros((LANES - USED, LAGS), f32)
    real, imag = 0.0, 0.0
    for i, left in enumerate((both, high)):
        cos, sin = base_ref[i, :SLOTS, :].astype(f32), base_ref[i, SLOTS:, :].astype(f32)
        coses = [cos, sign * cos, even * cos - odd * sin, even * cos + odd * sin, gap]
        sines = [sin, sign * sin, even * sin + odd * cos, even * sin - odd * cos, gap]
        for_real = jnp.concatenate(coses + [-item for item in sines], axis=0).astype(bf16)
        for_imag = jnp.concatenate(sines + coses, axis=0).astype(bf16)
        a, b = dot(left, for_real), dot(left, for_imag)
        real, imag = real + a[:count], imag + b[:count]
        if i == 0:
            real, imag = real + a[count:], imag + b[count:]
    turns = turns_ref[part_ref[0]]
    lags = real * turns[0:1] - imag * turns[1:2]
    for group in range(8):
        tile = lags[:, LANES * group : LANES * (group + 1)]
        for quarter in range(4):
            lane = slice(32 * quarter, 32 * (quarter + 1))
            out_ref[4 * group + quarter] = jnp.concatenate([tile[4 * c : 4 * c + 4, lane] for c in range(4)], axis=1)


def invert(parts):
    base, turns = inverse_tables()
    part = lax.axis_index("zl").astype(jnp.int32).reshape(1)
    return pl.pallas_call(
        inverse_kernel,
        out_shape=jax.ShapeDtypeStruct((32, 4, LANES), f32),
        in_specs=[SMEM, VMEM, VMEM, VMEM],
        out_specs=VMEM,
        compiler_params=pltpu.CompilerParams(vmem_limit_bytes=32 << 20),
        name="invert",
    )(part, parts, jnp.asarray(base), jnp.asarray(turns))


def exchange(value, axes):
    return lax.all_to_all(value, axes, split_axis=0, concat_axis=0, tiled=True)


def shards(records, source_ids, pair_rows, pair_bins, bin_places):
    spectra = make_spectra(records.reshape(CH_DEV, NT), pair_rows, pair_bins, bin_places.reshape(1, BINS))
    given = exchange(spectra, ("x", "zl")).reshape(CHANNELS, WIDE)
    parts = exchange(bin_pairs(given, source_ids).reshape(32, 16, WIDE), ("x", "y", "core"))
    shares = exchange(invert(parts).reshape(64, 2, LANES), ("x", "zl", "zh"))
    return jnp.sum(shares.reshape(4, 16, 2, LANES), axis=1).reshape(BIN_DEV, 32)


def solution(mesh):
    fine = Mesh(mesh.devices.reshape(4, 8, 4, 2, 2), ("x", "zl", "y", "zh", "core"))
    chan, tm = ("x", "zl"), ("y", "zh", "core")
    in_specs = (P(chan, tm, None), P(), P(None, chan), P(None, chan), P())
    return jax.shard_map(shards, mesh=fine, in_specs=in_specs, out_specs=P(tm, chan), check_vma=False)
```

time: 84.6 us -> 83.7 us (0.989)
  blocking collectives: 55.9 us -> 23 us
  waiting for transfers between devices: 8.98 us -> 27.7 us
  starting transfers between devices: 9.21 us -> 22.7 us
    all_to_all x3 -> x1, blocking collectives: 55.9 us -> 23 us  [exchange(): return lax.all_to_all(value, axes, split_axis=0, concat_axis=0, tiled=True)]
    all_to_all x1 -> x2, waiting for transfers between devices: 8.98 us -> 27.7 us  [exchange(): return lax.all_to_all(value, axes, split_axis=0, concat_axis=0, tiled=True)]
    all_to_all x1 -> x2, starting transfers between devices: 9.21 us -> 22.7 us  [exchange(): return lax.all_to_all(value, axes, split_axis=0, concat_axis=0, tiled=True)]
  transfers between devices with their start and end apart: 1 -> 2, of which waited for: 1 -> 2; matrix products, arithmetic and copies ran while one was open for 0% -> 0% of each run, Pallas kernels for 0% -> 0%
where the time goes in v2:
time: 83.7 us; the launch traced here: 83.4 us
  waiting for transfers between devices  27.7 us (33%)
  blocking collectives  23 us (27%)
  starting transfers between devices  22.7 us (27%)
  Pallas kernels  9.24 us (11%)
    all_to_all x2, waiting for transfers between devices, exchange(): return lax.all_to_all(value, axes, split_axis=0, concat_axis=0, tiled=True)  27.7 us
    all_to_all x1, blocking collectives, exchange(): return lax.all_to_all(value, axes, split_axis=0, concat_axis=0, tiled=True)  23 us
    all_to_all x2, starting transfers between devices, exchange(): return lax.all_to_all(value, axes, split_axis=0, concat_axis=0, tiled=True)  22.7 us
    pallas_call x1, Pallas kernels, bin_pairs(): pl.pallas_call(pairs_kernel, out_shape=jax.ShapeDtypeStruct((BINS, WIDE),...  5.8 us
    pallas_call x1, Pallas kernels, make_spectra(): pl.pallas_call(spectra_kernel, out_shape=jax.ShapeDtypeStruct((4 * PARTS,...  2.87 us
  transfers between devices with their start and end apart: 2, of which 2 were waited for; matrix products, arithmetic and copies ran while one was open for 0% of the time, Pallas kernels for 0%

profile of v2, /device:TPU:1, one launch (start us, length us, event | category | flops | bytes accessed | tf_op | source)
XLA Modules:
  0.0 83.4 jit_solution(17729651064902072998)
XLA Ops:
  0.0 0.0 copy-start.2
  0.0 2.9 %spectra.1 = bf16[32,16,256]{2,1,0:T(8,128)(2,1)} custom-call(bf16[16,768]{1,0:T(8,128)(2,1)} %bitcast.11, bf16[2,768,384]{2,1,0:T(8,128)(2,1)} %constant.33.clone.table_hbm, s32[2,512]{1,0:T(2,128)} %rows_hbm.1, s32[2,512]{1,0:T(2,128)} %bins_hbm.1, s32[1,512]{1,0:T(1,128)} %bitcast.12), custom_call_target="tpu_custom_call" | custom-call | tf_op jit(solution)/shard_map/spectra/pallas_call | solution.py:121
  2.9 0.0 copy-start
  2.9 0.0 copy-start.1
  2.9 16.1 %all-to-all-start = ((bf16[32,16,256]{2,1,0:T(8,128)(2,1)}), bf16[32,16,256]{2,1,0:T(8,128)(2,1)S(1)}, u32[]{:S(2)}, u32[]{:S(2)}) async-start(bf16[32,16,256]{2,1,0:T(8,128)(2,1)} %spectra.1), calls=%async_computation | async-start | bytes 524288 | tf_op jit(solution)/shard_map/all_to_all | solution.py:223
  19.0 18.7 %all-to-all-done = bf16[32,16,256]{2,1,0:T(8,128)(2,1)S(1)} async-done(((bf16[32,16,256]{2,1,0:T(8,128)(2,1)}), bf16[32,16,256]{2,1,0:T(8,128)(2,1)S(1)}, u32[]{:S(2)}, u32[]{:S(2)}) %all-to-all-start) | async-done | bytes 262176 | tf_op jit(solution)/shard_map/all_to_all | solution.py:223
  37.7 0.0 copy-done.2
  37.7 5.8 %bin_pairs.1 = bf16[512,256]{1,0:T(8,128)(2,1)} custom-call(s32[1]{0:T(128)} %bitcast.1.step_ref, bf16[512,256]{1,0:T(8,128)(2,1)S(1)} %bitcast.9, s32[2,128]{1,0:T(2,128)S(1)} %copy-done.2), custom_call_target="tpu_custom_call" | custom-call | tf_op jit(solution)/shard_map/bin_pairs/pallas_call | solution.py:167
  43.5 6.6 %all-to-all-start.1 = ((bf16[32,16,256]{2,1,0:T(8,128)(2,1)}), bf16[32,16,256]{2,1,0:T(8,128)(2,1)S(1)}, u32[]{:S(2)}, u32[]{:S(2)}) async-start(bf16[32,16,256]{2,1,0:T(8,128)(2,1)} %bitcast.5), calls=%async_computation.1 | async-start | bytes 524288 | tf_op jit(solution)/shard_map/all_to_all | solution.py:223
  50.2 9.0 %all-to-all-done.1.parts_ref = bf16[32,16,256]{2,1,0:T(8,128)(2,1)S(1)} async-done(((bf16[32,16,256]{2,1,0:T(8,128)(2,1)}), bf16[32,16,256]{2,1,0:T(8,128)(2,1)S(1)}, u32[]{:S(2)}, u32[]{:S(2)}) %all-to-all-start.1) | async-done | bytes 262176 | tf_op jit(solution)/shard_map/all_to_all | solution.py:223
  59.1 0.0 copy-done
  59.1 0.0 copy-done.1
  59.1 0.6 invert.1
  59.7 23.0 %all_to_all.15 = f32[64,2,128]{2,1,0:T(2,128)S(1)} all-to-all(f32[64,2,128]{2,1,0:T(2,128)S(1)} %bitcast.10), channel_id=1, replica_groups=mesh['x'=4,'zl'=8,'y'=4,'zh'=2,'core'=2] {'x','zl','zh'}, dimensions={0} | all-to-all | bytes 131072 | tf_op jit(solution)/shard_map/all_to_all | solution.py:223
  82.7 0.7 reshape.35
  (1 shorter events, 0.0 us)
Async XLA Ops:
  0.0 37.7 %copy-start.2 = (s32[2,128]{1,0:T(2,128)S(1)}, s32[2,128]{1,0:T(2,128)}, u32[]{:S(2)}) copy-start(s32[2,128]{1,0:T(2,128)} %ids_ref.1) | copy-start | bytes 3076
  2.9 56.3 %copy-start = (bf16[2,48,1024]{2,1,0:T(8,128)(2,1)S(1)}, bf16[2,48,1024]{2,1,0:T(8,128)(2,1)}, u32[]{:S(2)}) copy-start(bf16[2,48,1024]{2,1,0:T(8,128)(2,1)} %constant.34.clone.base_ref) | copy-start | bytes 589828
  2.9 56.3 %copy-start.1 = (f32[8,2,1024]{2,1,0:T(2,128)S(1)}, f32[8,2,1024]{2,1,0:T(2,128)}, u32[]{:S(2)}) copy-start(f32[8,2,1024]{2,1,0:T(2,128)} %constant.35.clone.turns_ref) | copy-start | bytes 196612
  2.9 34.8 %all-to-all-start = ((bf16[32,16,256]{2,1,0:T(8,128)(2,1)}), bf16[32,16,256]{2,1,0:T(8,128)(2,1)S(1)}, u32[]{:S(2)}, u32[]{:S(2)}) async-start(bf16[32,16,256]{2,1,0:T(8,128)(2,1)} %spectra.1), calls=%async_computation | async-start | bytes 524288 | tf_op jit(solution)/shard_map/all_to_all | solution.py:223
  43.5 15.6 %all-to-all-start.1 = ((bf16[32,16,256]{2,1,0:T(8,128)(2,1)}), bf16[32,16,256]{2,1,0:T(8,128)(2,1)S(1)}, u32[]{:S(2)}, u32[]{:S(2)}) async-start(bf16[32,16,256]{2,1,0:T(8,128)(2,1)} %bitcast.5), calls=%async_computation.1 | async-start | bytes 524288 | tf_op jit(solution)/shard_map/all_to_all | solution.py:223

commit v3 on v2

--- a/solution.py
+++ b/solution.py
@@ -29,7 +29,6 @@
 dot = functools.partial(jnp.dot, preferred_element_type=f32)
 HBM = pl.BlockSpec(memory_space=pltpu.MemorySpace.HBM)
 VMEM = pl.BlockSpec(memory_space=pltpu.VMEM)
-SMEM = pl.BlockSpec(memory_space=pltpu.SMEM)
 
 
 def iota(shape, axis):
@@ -118,6 +117,7 @@
 def make_spectra(records, rows, bins, places):
     table = jnp.asarray(forward_table())
     inputs = (rows, bins, places, records, table)
+    rows, bins, places, records, table = (pltpu.with_memory_space_constraint(item, pltpu.HBM) for item in inputs)
     return pl.pallas_call(
         spectra_kernel,
         out_shape=jax.ShapeDtypeStruct((4 * PARTS, CH_DEV, WIDE), bf16),
@@ -126,12 +126,13 @@
         scratch_shapes=[pltpu.VMEM(item.shape, item.dtype) for item in inputs] + [
             pltpu.SemaphoreType.DMA((4 + CUTS,))
         ],
+        compiler_params=pltpu.CompilerParams(vmem_limit_bytes=16 << 20),
         name="spectra",
     )(records, table, rows, bins, places)
 
 
-def pairs_kernel(step_ref, given_ref, ids_ref, out_ref, src_ref, total_ref):
-    ids = jnp.broadcast_to(ids_ref[pl.ds(step_ref[0], 1), :].astype(f32), (8, SRC)).T
+def pairs_kernel(given_ref, ids_ref, out_ref, src_ref, total_ref):
+    ids = jnp.broadcast_to(ids_ref[pl.ds(lax.axis_index("x") // 2, 1), :].astype(f32), (8, SRC)).T
     pick = (ids[:, 0:1] == iota((SRC, CHANNELS), 1).astype(f32)).astype(f32).astype(bf16)
     used = iota((SRC, WIDE), 1) % LANES < USED
     src_ref[...] = jnp.where(used, dot(pick, given_ref[...]), 0.0).astype(bf16)
@@ -163,19 +164,18 @@
 
 
 def bin_pairs(given, ids):
-    step = (lax.axis_index("x") // 2).astype(jnp.int32).reshape(1)
     return pl.pallas_call(
         pairs_kernel,
         out_shape=jax.ShapeDtypeStruct((BINS, WIDE), bf16),
-        in_specs=[SMEM, VMEM, VMEM],
+        in_specs=[VMEM, VMEM],
         out_specs=VMEM,
         scratch_shapes=[pltpu.VMEM((SRC, WIDE), bf16), pltpu.VMEM((BINS, WIDE), f32)],
         compiler_params=pltpu.CompilerParams(vmem_limit_bytes=32 << 20),
         name="bin_pairs",
-    )(step, given, ids)
-
-
-def inverse_kernel(part_ref, parts_ref, base_ref, turns_ref, out_ref):
+    )(given, ids)
+
+
+def inverse_kernel(parts_ref, base_ref, turns_ref, out_ref):
     spectrum = jnp.sum(parts_ref[...].astype(f32), axis=0)
     high = spectrum.astype(bf16)
     low = (spectrum - high.astype(f32)).astype(bf16)
@@ -197,7 +197,7 @@
         real, imag = real + a[:count], imag + b[:count]
         if i == 0:
             real, imag = real + a[count:], imag + b[count:]
-    turns = turns_ref[part_ref[0]]
+    turns = turns_ref[lax.axis_index("zl")]
     lags = real * turns[0:1] - imag * turns[1:2]
     for group in range(8):
         tile = lags[:, LANES * group : LANES * (group + 1)]
@@ -208,15 +208,14 @@
 
 def invert(parts):
     base, turns = inverse_tables()
-    part = lax.axis_index("zl").astype(jnp.int32).reshape(1)
     return pl.pallas_call(
         inverse_kernel,
         out_shape=jax.ShapeDtypeStruct((32, 4, LANES), f32),
-        in_specs=[SMEM, VMEM, VMEM, VMEM],
+        in_specs=[VMEM, VMEM, VMEM],
         out_specs=VMEM,
         compiler_params=pltpu.CompilerParams(vmem_limit_bytes=32 << 20),
         name="invert",
-    )(part, parts, jnp.asarray(base), jnp.asarray(turns))
+    )(parts, jnp.asarray(base), jnp.asarray(turns))
 
 
 def exchange(value, axes):

time: 83.7 us -> 81.7 us (0.976)
  blocking collectives: 23 us -> 72.8 us
  waiting for transfers between devices: 27.7 us -> 0 us
  starting transfers between devices: 22.7 us -> 0 us
  Pallas kernels: 9.24 us -> 7.84 us
    all_to_all x1 -> x3, blocking collectives: 23 us -> 72.8 us  [exchange(): return lax.all_to_all(value, axes, split_axis=0, concat_axis=0, tiled=True)]
    all_to_all x2 -> x0, waiting for transfers between devices: 27.7 us -> none  [exchange(): return lax.all_to_all(value, axes, split_axis=0, concat_axis=0, tiled=True)]
    all_to_all x2 -> x0, starting transfers between devices: 22.7 us -> none  [exchange(): return lax.all_to_all(value, axes, split_axis=0, concat_axis=0, tiled=True)]
  transfers between devices with their start and end apart: 2 -> 0, of which waited for: 2 -> 0; matrix products, arithmetic and copies ran while one was open for 0% -> 0% of each run, Pallas kernels for 0% -> 0%
where the time goes in v3:
time: 81.7 us; the launch traced here: 81.4 us
  blocking collectives  72.8 us (89%)
  Pallas kernels  7.84 us (10%)
    all_to_all x3, blocking collectives, exchange(): return lax.all_to_all(value, axes, split_axis=0, concat_axis=0, tiled=True)  72.8 us
    pallas_call x1, Pallas kernels, bin_pairs(): pl.pallas_call(pairs_kernel, out_shape=jax.ShapeDtypeStruct((BINS, WIDE),...  5.06 us
    pallas_call x1, Pallas kernels, make_spectra(): pl.pallas_call(spectra_kernel, out_shape=jax.ShapeDtypeStruct((4 * PARTS,...  2.21 us

profile of v3, /device:TPU:1, one launch (start us, length us, event | category | flops | bytes accessed | tf_op | source)
XLA Modules:
  0.0 81.4 jit_solution(2147314359186715293)
XLA Ops:
  0.0 0.0 copy-start.2
  0.0 0.0 copy-start
  0.0 0.0 copy-start.1
  0.0 2.2 %spectra.1 = bf16[32,16,256]{2,1,0:T(8,128)(2,1)S(1)} custom-call(bf16[16,768]{1,0:T(8,128)(2,1)} %bitcast.10, bf16[2,768,384]{2,1,0:T(8,128)(2,1)} %constant.8.clone.table_hbm, s32[2,512]{1,0:T(2,128)} %rows_hbm.1, s32[2,512]{1,0:T(2,128)} %bins_hbm.1, s32[1,512]{1,0:T(1,128)} %bitcast.11), custom_call_target="tpu_custom_call" | custom-call | tf_op jit(solution)/shard_map/spectra/pallas_call | solution.py:121
  2.2 34.5 %all_to_all.15 = bf16[32,16,256]{2,1,0:T(8,128)(2,1)S(1)} all-to-all(bf16[32,16,256]{2,1,0:T(8,128)(2,1)S(1)} %spectra.1), channel_id=1, replica_groups=mesh['x'=4,'zl'=8,'y'=4,'zh'=2,'core'=2] {'x','zl'}, dimensions={0} | all-to-all | bytes 524288 | tf_op jit(solution)/shard_map/all_to_all | solution.py:222
  36.7 0.0 copy-done.2
  36.7 5.1 %bin_pairs.1 = bf16[512,256]{1,0:T(8,128)(2,1)S(1)} custom-call(bf16[512,256]{1,0:T(8,128)(2,1)S(1)} %bitcast.7, s32[2,128]{1,0:T(2,128)S(1)} %copy-done.2), custom_call_target="tpu_custom_call" | custom-call | tf_op jit(solution)/shard_map/bin_pairs/pallas_call | solution.py:167
  41.8 15.4 %all_to_all.16.parts_ref = bf16[32,16,256]{2,1,0:T(8,128)(2,1)S(1)} all-to-all(bf16[32,16,256]{2,1,0:T(8,128)(2,1)S(1)} %bitcast.8), channel_id=1, replica_groups=mesh['x'=4,'zl'=8,'y'=4,'zh'=2,'core'=2] {'x','y','core'}, dimensions={0} | all-to-all | bytes 524288 | tf_op jit(solution)/shard_map/all_to_all | solution.py:222
  57.2 0.0 copy-done
  57.2 0.0 copy-done.1
  57.2 0.6 invert.1
  57.8 23.0 %all_to_all.17 = f32[64,2,128]{2,1,0:T(2,128)S(1)} all-to-all(f32[64,2,128]{2,1,0:T(2,128)S(1)} %bitcast.9), channel_id=1, replica_groups=mesh['x'=4,'zl'=8,'y'=4,'zh'=2,'core'=2] {'x','zl','zh'}, dimensions={0} | all-to-all | bytes 131072 | tf_op jit(solution)/shard_map/all_to_all | solution.py:222
  80.8 0.7 reshape.27
  (1 shorter events, 0.0 us)
Async XLA Ops:
  0.0 36.7 %copy-start.2 = (s32[2,128]{1,0:T(2,128)S(1)}, s32[2,128]{1,0:T(2,128)}, u32[]{:S(2)}) copy-start(s32[2,128]{1,0:T(2,128)} %ids_ref.1) | copy-start | bytes 3076
  0.0 57.2 %copy-start = (bf16[2,48,1024]{2,1,0:T(8,128)(2,1)S(1)}, bf16[2,48,1024]{2,1,0:T(8,128)(2,1)}, u32[]{:S(2)}) copy-start(bf16[2,48,1024]{2,1,0:T(8,128)(2,1)} %constant.9.clone.base_ref) | copy-start | bytes 589828
  0.0 57.2 %copy-start.1 = (f32[8,2,1024]{2,1,0:T(2,128)S(1)}, f32[8,2,1024]{2,1,0:T(2,128)}, u32[]{:S(2)}) copy-start(f32[8,2,1024]{2,1,0:T(2,128)} %constant.10.clone.turns_ref) | copy-start | bytes 196612

commit v4 on v3

--- a/solution.py
+++ b/solution.py
@@ -73,8 +73,7 @@
 
     place = places_ref[...]
     owner, slot = place // BIN_DEV, place % BIN_DEV
-    order = (slot // 8) * 128 + (owner // 4) * 32 + (owner % 2) * 16
-    order = order + (slot % 4) * 4 + ((owner // 2) % 2) * 2 + (slot // 4) % 2
+    order = (owner // 4) * 128 + (owner % 2) * 64 + ((owner // 2) % 2) * 32 + (slot % 4) * 8 + slot // 4
     digits = jnp.broadcast_to(order - BINS // 2, (8, BINS)).astype(f32).astype(bf16)
     bins = jnp.concatenate([bins_ref[0:1, :], bins_ref[1:2, :]], axis=1)
     spots = dot(digits, (iota((BINS, PAIRS), 0) == bins).astype(f32).astype(bf16))[0:1]
@@ -129,6 +128,25 @@
         compiler_params=pltpu.CompilerParams(vmem_limit_bytes=16 << 20),
         name="spectra",
     )(records, table, rows, bins, places)
+
+
+def pack(total, out_ref):
+    for i in range(8):
+        kept, moved = total[64 * i : 64 * i + 48], total[64 * i + 48 : 64 * i + 64]
+        tiles = []
+        for start in (0, LANES):
+            thirds = [moved[:, start + 32 * k : start + 32 * (k + 1)] for k in range(3)]
+            tiles += [kept[:, start : start + USED], jnp.concatenate(thirds, axis=0)]
+        out_ref[i] = jnp.concatenate(tiles, axis=1).astype(bf16)
+
+
+def unpack(packed):
+    moved = []
+    for start in (0, LANES):
+        spare = packed[:, start + USED : start + LANES]
+        thirds = [spare[16 * k : 16 * (k + 1)] for k in range(3)]
+        moved += thirds + [jnp.zeros((16, LANES - USED), f32)]
+    return jnp.concatenate([packed, jnp.concatenate(moved, axis=1)], axis=0)
 
 
 def pairs_kernel(given_ref, ids_ref, out_ref, src_ref, total_ref):
@@ -158,7 +176,7 @@
             if half == 0 and group == 0:
                 total_ref[...] = part
             elif half == 1 and group == 3:
-                out_ref[...] = (total_ref[...] + part).astype(bf16)
+                pack(total_ref[...] + part, out_ref)
             else:
                 total_ref[...] += part
 
@@ -166,7 +184,7 @@
 def bin_pairs(given, ids):
     return pl.pallas_call(
         pairs_kernel,
-        out_shape=jax.ShapeDtypeStruct((BINS, WIDE), bf16),
+        out_shape=jax.ShapeDtypeStruct((8, 48, WIDE), bf16),
         in_specs=[VMEM, VMEM],
         out_specs=VMEM,
         scratch_shapes=[pltpu.VMEM((SRC, WIDE), bf16), pltpu.VMEM((BINS, WIDE), f32)],
@@ -176,7 +194,7 @@
 
 
 def inverse_kernel(parts_ref, base_ref, turns_ref, out_ref):
-    spectrum = jnp.sum(parts_ref[...].astype(f32), axis=0)
+    spectrum = unpack(jnp.sum(parts_ref[...].astype(f32), axis=0))
     high = spectrum.astype(bf16)
     low = (spectrum - high.astype(f32)).astype(bf16)
     both = jnp.concatenate([high, low], axis=0)
@@ -199,18 +217,20 @@
             real, imag = real + a[count:], imag + b[count:]
     turns = turns_ref[lax.axis_index("zl")]
     lags = real * turns[0:1] - imag * turns[1:2]
-    for group in range(8):
-        tile = lags[:, LANES * group : LANES * (group + 1)]
-        for quarter in range(4):
-            lane = slice(32 * quarter, 32 * (quarter + 1))
-            out_ref[4 * group + quarter] = jnp.concatenate([tile[4 * c : 4 * c + 4, lane] for c in range(4)], axis=1)
+    for zh in range(2):
+        for group in range(8):
+            tile = lags[32 * zh : 32 * (zh + 1), LANES * group : LANES * (group + 1)]
+            for quarter in range(4):
+                lane = slice(32 * quarter, 32 * (quarter + 1))
+                pieces = [tile[8 * c : 8 * c + 8, lane] for c in range(4)]
+                out_ref[8 * group + 2 * quarter + zh] = jnp.concatenate(pieces, axis=1).astype(bf16)
 
 
 def invert(parts):
     base, turns = inverse_tables()
     return pl.pallas_call(
         inverse_kernel,
-        out_shape=jax.ShapeDtypeStruct((32, 4, LANES), f32),
+        out_shape=jax.ShapeDtypeStruct((64, 8, LANES), bf16),
         in_specs=[VMEM, VMEM, VMEM],
         out_specs=VMEM,
         compiler_params=pltpu.CompilerParams(vmem_limit_bytes=32 << 20),
@@ -225,9 +245,9 @@
 def shards(records, source_ids, pair_rows, pair_bins, bin_places):
     spectra = make_spectra(records.reshape(CH_DEV, NT), pair_rows, pair_bins, bin_places.reshape(1, BINS))
     given = exchange(spectra, ("x", "zl")).reshape(CHANNELS, WIDE)
-    parts = exchange(bin_pairs(given, source_ids).reshape(32, 16, WIDE), ("x", "y", "core"))
-    shares = exchange(invert(parts).reshape(64, 2, LANES), ("x", "zl", "zh"))
-    return jnp.sum(shares.reshape(4, 16, 2, LANES), axis=1).reshape(BIN_DEV, 32)
+    parts = exchange(bin_pairs(given, source_ids), ("y", "core"))
+    shares = exchange(invert(parts), ("x", "zl", "zh"))
+    return jnp.sum(shares.astype(f32), axis=0).reshape(BIN_DEV, 32)
 
 
 def solution(mesh):

time: 81.7 us -> 80.5 us (0.985); the launches traced: 81.4 us -> 79.2 us
  blocking collectives: 72.8 us -> 70.3 us
    all_to_all x3, blocking collectives: 72.8 us -> 70.3 us  [exchange(): return lax.all_to_all(value, axes, split_axis=0, concat_axis=0, tiled=True)]
where the time goes in v4:
time: 80.5 us; the launch traced here: 79.2 us
  blocking collectives  70.3 us (87%)
  Pallas kernels  8.04 us (10%)
    all_to_all x3, blocking collectives, exchange(): return lax.all_to_all(value, axes, split_axis=0, concat_axis=0, tiled=True)  70.3 us
    pallas_call x1, Pallas kernels, bin_pairs(): pl.pallas_call(pairs_kernel, out_shape=jax.ShapeDtypeStruct((8, 48, WIDE)...  5.2 us
    pallas_call x1, Pallas kernels, make_spectra(): pl.pallas_call(spectra_kernel, out_shape=jax.ShapeDtypeStruct((4 * PARTS,...  2.2 us

profile of v4, /device:TPU:1, one launch (start us, length us, event | category | flops | bytes accessed | tf_op | source)
XLA Modules:
  0.0 79.2 jit_solution(5908895849013161416)
XLA Ops:
  0.0 0.0 copy-start.2
  0.0 0.0 copy-start
  0.0 0.0 copy-start.1
  0.0 2.2 %spectra.1 = bf16[32,16,256]{2,1,0:T(8,128)(2,1)S(1)} custom-call(bf16[16,768]{1,0:T(8,128)(2,1)} %bitcast.4, bf16[2,768,384]{2,1,0:T(8,128)(2,1)} %constant.8.clone.table_hbm, s32[2,512]{1,0:T(2,128)} %rows_hbm.1, s32[2,512]{1,0:T(2,128)} %bins_hbm.1, s32[1,512]{1,0:T(1,128)} %bitcast.5), custom_call_target="tpu_custom_call" | custom-call | tf_op jit(solution)/shard_map/spectra/pallas_call | solution.py:120
  2.2 34.5 %all_to_all.15 = bf16[32,16,256]{2,1,0:T(8,128)(2,1)S(1)} all-to-all(bf16[32,16,256]{2,1,0:T(8,128)(2,1)S(1)} %spectra.1), channel_id=1, replica_groups=mesh['x'=4,'zl'=8,'y'=4,'zh'=2,'core'=2] {'x','zl'}, dimensions={0} | all-to-all | bytes 524288 | tf_op jit(solution)/shard_map/all_to_all | solution.py:242
  36.7 0.0 copy-done.2
  36.7 5.2 %bin_pairs.1 = bf16[8,48,256]{2,1,0:T(8,128)(2,1)S(1)} custom-call(bf16[512,256]{1,0:T(8,128)(2,1)S(1)} %bitcast.3, s32[2,128]{1,0:T(2,128)S(1)} %copy-done.2), custom_call_target="tpu_custom_call" | custom-call | tf_op jit(solution)/shard_map/bin_pairs/pallas_call | solution.py:185
  41.9 11.9 %all_to_all.16.parts_ref = bf16[8,48,256]{2,1,0:T(8,128)(2,1)S(1)} all-to-all(bf16[8,48,256]{2,1,0:T(8,128)(2,1)S(1)} %bin_pairs.1), channel_id=1, replica_groups=mesh['x'=4,'zl'=8,'y'=4,'zh'=2,'core'=2] {'y','core'}, dimensions={0} | all-to-all | bytes 393216 | tf_op jit(solution)/shard_map/all_to_all | solution.py:242
  53.8 0.0 copy-done
  53.8 0.0 copy-done.1
  53.8 0.6 invert.1
  54.5 24.0 %all_to_all.17 = bf16[64,8,128]{2,1,0:T(8,128)(2,1)S(1)} all-to-all(bf16[64,8,128]{2,1,0:T(8,128)(2,1)S(1)} %invert.1), channel_id=1, replica_groups=mesh['x'=4,'zl'=8,'y'=4,'zh'=2,'core'=2] {'x','zl','zh'}, dimensions={0} | all-to-all | bytes 262144 | tf_op jit(solution)/shard_map/all_to_all | solution.py:242
  78.4 0.1 convert_reduce_fusion
  78.5 0.7 reshape.15
Async XLA Ops:
  0.0 36.7 %copy-start.2 = (s32[2,128]{1,0:T(2,128)S(1)}, s32[2,128]{1,0:T(2,128)}, u32[]{:S(2)}) copy-start(s32[2,128]{1,0:T(2,128)} %ids_ref.1) | copy-start | bytes 3076
  0.0 53.8 %copy-start = (bf16[2,48,1024]{2,1,0:T(8,128)(2,1)S(1)}, bf16[2,48,1024]{2,1,0:T(8,128)(2,1)}, u32[]{:S(2)}) copy-start(bf16[2,48,1024]{2,1,0:T(8,128)(2,1)} %constant.9.clone.base_ref) | copy-start | bytes 589828
  0.0 53.8 %copy-start.1 = (f32[8,2,1024]{2,1,0:T(2,128)S(1)}, f32[8,2,1024]{2,1,0:T(2,128)}, u32[]{:S(2)}) copy-start(f32[8,2,1024]{2,1,0:T(2,128)} %constant.10.clone.turns_ref) | copy-start | bytes 196612

commit v5 on v4

--- a/solution.py
+++ b/solution.py
@@ -110,7 +110,7 @@
         for x in range(4):
             rows_x = slice(CH_DEV * x, CH_DEV * (x + 1))
             full = jnp.concatenate([parts[0] + lists_1[rows_x], parts[1] + lists_2[rows_x]], axis=1)
-            out_ref[PARTS * x + z] = full.astype(bf16)
+            out_ref[4 * z + x] = full.astype(bf16)
 
 
 def make_spectra(records, rows, bins, places):
@@ -150,7 +150,10 @@
 
 
 def pairs_kernel(given_ref, ids_ref, out_ref, src_ref, total_ref):
-    ids = jnp.broadcast_to(ids_ref[pl.ds(lax.axis_index("x") // 2, 1), :].astype(f32), (8, SRC)).T
+    ids = ids_ref[pl.ds(lax.axis_index("x") // 2, 1), :]
+    block = ids // CH_DEV
+    ids = (block % PARTS * 4 + block // PARTS) * CH_DEV + ids % CH_DEV
+    ids = jnp.broadcast_to(ids.astype(f32), (8, SRC)).T
     pick = (ids[:, 0:1] == iota((SRC, CHANNELS), 1).astype(f32)).astype(f32).astype(bf16)
     used = iota((SRC, WIDE), 1) % LANES < USED
     src_ref[...] = jnp.where(used, dot(pick, given_ref[...]), 0.0).astype(bf16)
@@ -223,7 +226,7 @@
             for quarter in range(4):
                 lane = slice(32 * quarter, 32 * (quarter + 1))
                 pieces = [tile[8 * c : 8 * c + 8, lane] for c in range(4)]
-                out_ref[8 * group + 2 * quarter + zh] = jnp.concatenate(pieces, axis=1).astype(bf16)
+                out_ref[32 * zh + 4 * ((4 * group + quarter) % 8) + group // 2] = jnp.concatenate(pieces, axis=1).astype(bf16)
 
 
 def invert(parts):
@@ -244,9 +247,9 @@
 
 def shards(records, source_ids, pair_rows, pair_bins, bin_places):
     spectra = make_spectra(records.reshape(CH_DEV, NT), pair_rows, pair_bins, bin_places.reshape(1, BINS))
-    given = exchange(spectra, ("x", "zl")).reshape(CHANNELS, WIDE)
+    given = exchange(spectra, ("zl", "x")).reshape(CHANNELS, WIDE)
     parts = exchange(bin_pairs(given, source_ids), ("y", "core"))
-    shares = exchange(invert(parts), ("x", "zl", "zh"))
+    shares = exchange(invert(parts), ("zh", "zl", "x"))
     return jnp.sum(shares.astype(f32), axis=0).reshape(BIN_DEV, 32)
 
 

time: 80.5 us -> 79.6 us (0.989)
  no operation moved by 1% of the time
where the time goes in v5:
time: 79.6 us; the launch traced here: 78.4 us
  blocking collectives  69.6 us (87%)
  Pallas kernels  8.07 us (10%)
    all_to_all x3, blocking collectives, exchange(): return lax.all_to_all(value, axes, split_axis=0, concat_axis=0, tiled=True)  69.6 us
    pallas_call x1, Pallas kernels, bin_pairs(): pl.pallas_call(pairs_kernel, out_shape=jax.ShapeDtypeStruct((8, 48, WIDE)...  5.22 us
    pallas_call x1, Pallas kernels, make_spectra(): pl.pallas_call(spectra_kernel, out_shape=jax.ShapeDtypeStruct((4 * PARTS,...  2.2 us

profile of v5, /device:TPU:1, one launch (start us, length us, event | category | flops | bytes accessed | tf_op | source)
XLA Modules:
  0.0 78.4 jit_solution(11397083221154109050)
XLA Ops:
  0.0 0.0 copy-start.2
  0.0 0.0 copy-start
  0.0 0.0 copy-start.1
  0.0 2.2 %spectra.1 = bf16[32,16,256]{2,1,0:T(8,128)(2,1)S(1)} custom-call(bf16[16,768]{1,0:T(8,128)(2,1)} %bitcast.4, bf16[2,768,384]{2,1,0:T(8,128)(2,1)} %constant.8.clone.table_hbm, s32[2,512]{1,0:T(2,128)} %rows_hbm.1, s32[2,512]{1,0:T(2,128)} %bins_hbm.1, s32[1,512]{1,0:T(1,128)} %bitcast.5), custom_call_target="tpu_custom_call" | custom-call | tf_op jit(solution)/shard_map/spectra/pallas_call | solution.py:120
  2.2 32.5 %all_to_all.15 = bf16[32,16,256]{2,1,0:T(8,128)(2,1)S(1)} all-to-all(bf16[32,16,256]{2,1,0:T(8,128)(2,1)S(1)} %spectra.1), channel_id=1, replica_groups=mesh['x'=4,'zl'=8,'y'=4,'zh'=2,'core'=2] {'zl','x'}, dimensions={0} | all-to-all | bytes 524288 | tf_op jit(solution)/shard_map/all_to_all | solution.py:245
  34.7 0.0 copy-done.2
  34.7 5.2 %bin_pairs.1 = bf16[8,48,256]{2,1,0:T(8,128)(2,1)S(1)} custom-call(bf16[512,256]{1,0:T(8,128)(2,1)S(1)} %bitcast.3, s32[2,128]{1,0:T(2,128)S(1)} %copy-done.2), custom_call_target="tpu_custom_call" | custom-call | tf_op jit(solution)/shard_map/bin_pairs/pallas_call | solution.py:188
  39.9 13.6 %all_to_all.16.parts_ref = bf16[8,48,256]{2,1,0:T(8,128)(2,1)S(1)} all-to-all(bf16[8,48,256]{2,1,0:T(8,128)(2,1)S(1)} %bin_pairs.1), channel_id=1, replica_groups=mesh['x'=4,'zl'=8,'y'=4,'zh'=2,'core'=2] {'y','core'}, dimensions={0} | all-to-all | bytes 393216 | tf_op jit(solution)/shard_map/all_to_all | solution.py:245
  53.5 0.0 copy-done
  53.5 0.0 copy-done.1
  53.5 0.6 invert.1
  54.2 23.5 %all_to_all.17 = bf16[64,8,128]{2,1,0:T(8,128)(2,1)S(1)} all-to-all(bf16[64,8,128]{2,1,0:T(8,128)(2,1)S(1)} %invert.1), channel_id=1, replica_groups=mesh['x'=4,'zl'=8,'y'=4,'zh'=2,'core'=2] {'zh','zl','x'}, dimensions={0} | all-to-all | bytes 262144 | tf_op jit(solution)/shard_map/all_to_all | solution.py:245
  77.7 0.1 convert_reduce_fusion
  77.8 0.7 reshape.15
Async XLA Ops:
  0.0 34.7 %copy-start.2 = (s32[2,128]{1,0:T(2,128)S(1)}, s32[2,128]{1,0:T(2,128)}, u32[]{:S(2)}) copy-start(s32[2,128]{1,0:T(2,128)} %ids_ref.1) | copy-start | bytes 3076
  0.0 53.5 %copy-start = (bf16[2,48,1024]{2,1,0:T(8,128)(2,1)S(1)}, bf16[2,48,1024]{2,1,0:T(8,128)(2,1)}, u32[]{:S(2)}) copy-start(bf16[2,48,1024]{2,1,0:T(8,128)(2,1)} %constant.9.clone.base_ref) | copy-start | bytes 589828
  0.0 53.5 %copy-start.1 = (f32[8,2,1024]{2,1,0:T(2,128)S(1)}, f32[8,2,1024]{2,1,0:T(2,128)}, u32[]{:S(2)}) copy-start(f32[8,2,1024]{2,1,0:T(2,128)} %constant.10.clone.turns_ref) | copy-start | bytes 196612

commit v6 on v5

--- a/solution.py
+++ b/solution.py
@@ -73,10 +73,12 @@
 
     place = places_ref[...]
     owner, slot = place // BIN_DEV, place % BIN_DEV
-    order = (owner // 4) * 128 + (owner % 2) * 64 + ((owner // 2) % 2) * 32 + (slot % 4) * 8 + slot // 4
+    order = (owner % 2) * 256 + (owner // 4) * 64 + ((owner // 2) % 2) * 32 + (slot % 4) * 8 + slot // 4
     digits = jnp.broadcast_to(order - BINS // 2, (8, BINS)).astype(f32).astype(bf16)
-    bins = jnp.concatenate([bins_ref[0:1, :], bins_ref[1:2, :]], axis=1)
-    spots = dot(digits, (iota((BINS, PAIRS), 0) == bins).astype(f32).astype(bf16))[0:1]
+    bins = (jnp.concatenate([bins_ref[0:1, :], bins_ref[1:2, :]], axis=1) - BINS // 2).astype(f32).astype(bf16)
+    each = (iota((BINS, PAIRS), 0) - BINS // 2).astype(f32).astype(bf16)
+    match = jnp.where(each == bins, jnp.ones((BINS, PAIRS), bf16), jnp.zeros((BINS, PAIRS), bf16))
+    spots = dot(digits, match)[0:1]
     rows = jnp.concatenate([rows_ref[0:1, :], rows_ref[1:2, :]], axis=1)
 
     chosen = iota((PAIRS // 16, PAIRS), 0) == iota((PAIRS // 16, PAIRS), 1) // 16
@@ -248,7 +250,7 @@
 def shards(records, source_ids, pair_rows, pair_bins, bin_places):
     spectra = make_spectra(records.reshape(CH_DEV, NT), pair_rows, pair_bins, bin_places.reshape(1, BINS))
     given = exchange(spectra, ("zl", "x")).reshape(CHANNELS, WIDE)
-    parts = exchange(bin_pairs(given, source_ids), ("y", "core"))
+    parts = exchange(bin_pairs(given, source_ids), ("core", "y"))
     shares = exchange(invert(parts), ("zh", "zl", "x"))
     return jnp.sum(shares.astype(f32), axis=0).reshape(BIN_DEV, 32)
 

time: 79.6 us -> 79.8 us (level)
  no operation moved by 1% of the time
where the time goes in v6:
time: 79.8 us; the launch traced here: 78.3 us
  blocking collectives  69.6 us (87%)
  Pallas kernels  7.93 us (10%)
    all_to_all x3, blocking collectives, exchange(): return lax.all_to_all(value, axes, split_axis=0, concat_axis=0, tiled=True)  69.6 us
    pallas_call x1, Pallas kernels, bin_pairs(): pl.pallas_call(pairs_kernel, out_shape=jax.ShapeDtypeStruct((8, 48, WIDE)...  5.22 us
    pallas_call x1, Pallas kernels, make_spectra(): pl.pallas_call(spectra_kernel, out_shape=jax.ShapeDtypeStruct((4 * PARTS,...  2.07 us

profile of v6, /device:TPU:1, one launch (start us, length us, event | category | flops | bytes accessed | tf_op | source)
XLA Modules:
  0.0 78.3 jit_solution(17729859818747221492)
XLA Ops:
  0.0 0.0 copy-start.2
  0.0 0.0 copy-start
  0.0 0.0 copy-start.1
  0.0 2.1 %spectra.1 = bf16[32,16,256]{2,1,0:T(8,128)(2,1)S(1)} custom-call(bf16[16,768]{1,0:T(8,128)(2,1)} %bitcast.4, bf16[2,768,384]{2,1,0:T(8,128)(2,1)} %constant.8.clone.table_hbm, s32[2,512]{1,0:T(2,128)} %rows_hbm.1, s32[2,512]{1,0:T(2,128)} %bins_hbm.1, s32[1,512]{1,0:T(1,128)} %bitcast.5), custom_call_target="tpu_custom_call" | custom-call | tf_op jit(solution)/shard_map/spectra/pallas_call | solution.py:122
  2.1 32.5 %all_to_all.15 = bf16[32,16,256]{2,1,0:T(8,128)(2,1)S(1)} all-to-all(bf16[32,16,256]{2,1,0:T(8,128)(2,1)S(1)} %spectra.1), channel_id=1, replica_groups=mesh['x'=4,'zl'=8,'y'=4,'zh'=2,'core'=2] {'zl','x'}, dimensions={0} | all-to-all | bytes 524288 | tf_op jit(solution)/shard_map/all_to_all | solution.py:247
  34.6 0.0 copy-done.2
  34.6 5.2 %bin_pairs.1 = bf16[8,48,256]{2,1,0:T(8,128)(2,1)S(1)} custom-call(bf16[512,256]{1,0:T(8,128)(2,1)S(1)} %bitcast.3, s32[2,128]{1,0:T(2,128)S(1)} %copy-done.2), custom_call_target="tpu_custom_call" | custom-call | tf_op jit(solution)/shard_map/bin_pairs/pallas_call | solution.py:190
  39.8 13.6 %all_to_all.16.parts_ref = bf16[8,48,256]{2,1,0:T(8,128)(2,1)S(1)} all-to-all(bf16[8,48,256]{2,1,0:T(8,128)(2,1)S(1)} %bin_pairs.1), channel_id=1, replica_groups=mesh['x'=4,'zl'=8,'y'=4,'zh'=2,'core'=2] {'core','y'}, dimensions={0} | all-to-all | bytes 393216 | tf_op jit(solution)/shard_map/all_to_all | solution.py:247
  53.4 0.0 copy-done
  53.4 0.0 copy-done.1
  53.4 0.6 invert.1
  54.1 23.5 %all_to_all.17 = bf16[64,8,128]{2,1,0:T(8,128)(2,1)S(1)} all-to-all(bf16[64,8,128]{2,1,0:T(8,128)(2,1)S(1)} %invert.1), channel_id=1, replica_groups=mesh['x'=4,'zl'=8,'y'=4,'zh'=2,'core'=2] {'zh','zl','x'}, dimensions={0} | all-to-all | bytes 262144 | tf_op jit(solution)/shard_map/all_to_all | solution.py:247
  77.6 0.1 convert_reduce_fusion
  77.6 0.7 reshape.15
Async XLA Ops:
  0.0 34.6 %copy-start.2 = (s32[2,128]{1,0:T(2,128)S(1)}, s32[2,128]{1,0:T(2,128)}, u32[]{:S(2)}) copy-start(s32[2,128]{1,0:T(2,128)} %ids_ref.1) | copy-start | bytes 3076
  0.0 53.4 %copy-start = (bf16[2,48,1024]{2,1,0:T(8,128)(2,1)S(1)}, bf16[2,48,1024]{2,1,0:T(8,128)(2,1)}, u32[]{:S(2)}) copy-start(bf16[2,48,1024]{2,1,0:T(8,128)(2,1)} %constant.9.clone.base_ref) | copy-start | bytes 589828
  0.0 53.4 %copy-start.1 = (f32[8,2,1024]{2,1,0:T(2,128)S(1)}, f32[8,2,1024]{2,1,0:T(2,128)}, u32[]{:S(2)}) copy-start(f32[8,2,1024]{2,1,0:T(2,128)} %constant.10.clone.turns_ref) | copy-start | bytes 196612

commit v7 on v5

--- a/solution.py
+++ b/solution.py
@@ -73,7 +73,7 @@
 
     place = places_ref[...]
     owner, slot = place // BIN_DEV, place % BIN_DEV
-    order = (owner // 4) * 128 + (owner % 2) * 64 + ((owner // 2) % 2) * 32 + (slot % 4) * 8 + slot // 4
+    order = (owner // 4) * 128 + (owner % 2) * 64 + ((owner // 2) % 2) * 32 + slot
     digits = jnp.broadcast_to(order - BINS // 2, (8, BINS)).astype(f32).astype(bf16)
     bins = jnp.concatenate([bins_ref[0:1, :], bins_ref[1:2, :]], axis=1)
     spots = dot(digits, (iota((BINS, PAIRS), 0) == bins).astype(f32).astype(bf16))[0:1]
@@ -241,6 +241,23 @@
     )(parts, jnp.asarray(base), jnp.asarray(turns))
 
 
+def sum_kernel(shares_ref, out_ref):
+    total = jnp.sum(shares_ref[...].astype(f32), axis=0)
+    for c in range(4):
+        out_ref[8 * c : 8 * c + 8, :] = total[:, 32 * c : 32 * c + 32]
+
+
+def sum_shares(shares):
+    return pl.pallas_call(
+        sum_kernel,
+        out_shape=jax.ShapeDtypeStruct((BIN_DEV, 32), f32),
+        in_specs=[VMEM],
+        out_specs=VMEM,
+        compiler_params=pltpu.CompilerParams(vmem_limit_bytes=16 << 20),
+        name="sum_shares",
+    )(shares)
+
+
 def exchange(value, axes):
     return lax.all_to_all(value, axes, split_axis=0, concat_axis=0, tiled=True)
 
@@ -249,8 +266,7 @@
     spectra = make_spectra(records.reshape(CH_DEV, NT), pair_rows, pair_bins, bin_places.reshape(1, BINS))
     given = exchange(spectra, ("zl", "x")).reshape(CHANNELS, WIDE)
     parts = exchange(bin_pairs(given, source_ids), ("y", "core"))
-    shares = exchange(invert(parts), ("zh", "zl", "x"))
-    return jnp.sum(shares.astype(f32), axis=0).reshape(BIN_DEV, 32)
+    return sum_shares(exchange(invert(parts), ("zh", "zl", "x")))
 
 
 def solution(mesh):

time: 79.6 us -> 79.6 us (level)
  no operation moved by 1% of the time
where the time goes in v7:
time: 79.6 us; the launch traced here: 78.2 us
  blocking collectives  69.4 us (87%)
  Pallas kernels  8.8 us (11%)
    all_to_all x3, blocking collectives, exchange(): return lax.all_to_all(value, axes, split_axis=0, concat_axis=0, tiled=True)  69.4 us
    pallas_call x1, Pallas kernels, bin_pairs(): pl.pallas_call(pairs_kernel, out_shape=jax.ShapeDtypeStruct((8, 48, WIDE)...  5.22 us
    pallas_call x1, Pallas kernels, make_spectra(): pl.pallas_call(spectra_kernel, out_shape=jax.ShapeDtypeStruct((4 * PARTS,...  2.2 us

profile of v7, /device:TPU:1, one launch (start us, length us, event | category | flops | bytes accessed | tf_op | source)
XLA Modules:
  0.0 78.2 jit_solution(2758745044867082029)
XLA Ops:
  0.0 0.0 copy-start.2
  0.0 0.0 copy-start
  0.0 0.0 copy-start.1
  0.0 2.2 %spectra.1 = bf16[32,16,256]{2,1,0:T(8,128)(2,1)S(1)} custom-call(bf16[16,768]{1,0:T(8,128)(2,1)} %bitcast.4, bf16[2,768,384]{2,1,0:T(8,128)(2,1)} %constant.6.clone.table_hbm, s32[2,512]{1,0:T(2,128)} %rows_hbm.1, s32[2,512]{1,0:T(2,128)} %bins_hbm.1, s32[1,512]{1,0:T(1,128)} %bitcast.5), custom_call_target="tpu_custom_call" | custom-call | tf_op jit(solution)/shard_map/spectra/pallas_call | solution.py:120
  2.2 32.5 %all_to_all.15 = bf16[32,16,256]{2,1,0:T(8,128)(2,1)S(1)} all-to-all(bf16[32,16,256]{2,1,0:T(8,128)(2,1)S(1)} %spectra.1), channel_id=1, replica_groups=mesh['x'=4,'zl'=8,'y'=4,'zh'=2,'core'=2] {'zl','x'}, dimensions={0} | all-to-all | bytes 524288 | tf_op jit(solution)/shard_map/all_to_all | solution.py:262
  34.7 0.0 copy-done.2
  34.7 5.2 %bin_pairs.1 = bf16[8,48,256]{2,1,0:T(8,128)(2,1)S(1)} custom-call(bf16[512,256]{1,0:T(8,128)(2,1)S(1)} %bitcast.3, s32[2,128]{1,0:T(2,128)S(1)} %copy-done.2), custom_call_target="tpu_custom_call" | custom-call | tf_op jit(solution)/shard_map/bin_pairs/pallas_call | solution.py:188
  39.9 13.6 %all_to_all.16.parts_ref = bf16[8,48,256]{2,1,0:T(8,128)(2,1)S(1)} all-to-all(bf16[8,48,256]{2,1,0:T(8,128)(2,1)S(1)} %bin_pairs.1), channel_id=1, replica_groups=mesh['x'=4,'zl'=8,'y'=4,'zh'=2,'core'=2] {'y','core'}, dimensions={0} | all-to-all | bytes 393216 | tf_op jit(solution)/shard_map/all_to_all | solution.py:262
  53.5 0.0 copy-done
  53.5 0.0 copy-done.1
  53.5 0.6 invert.1
  54.2 23.3 %all_to_all.17.shares_ref = bf16[64,8,128]{2,1,0:T(8,128)(2,1)S(1)} all-to-all(bf16[64,8,128]{2,1,0:T(8,128)(2,1)S(1)} %invert.1), channel_id=1, replica_groups=mesh['x'=4,'zl'=8,'y'=4,'zh'=2,'core'=2] {'zh','zl','x'}, dimensions={0} | all-to-all | bytes 262144 | tf_op jit(solution)/shard_map/all_to_all | solution.py:262
  77.5 0.7 sum_shares.1
Async XLA Ops:
  0.0 34.7 %copy-start.2 = (s32[2,128]{1,0:T(2,128)S(1)}, s32[2,128]{1,0:T(2,128)}, u32[]{:S(2)}) copy-start(s32[2,128]{1,0:T(2,128)} %ids_ref.1) | copy-start | bytes 3076
  0.0 53.5 %copy-start = (bf16[2,48,1024]{2,1,0:T(8,128)(2,1)S(1)}, bf16[2,48,1024]{2,1,0:T(8,128)(2,1)}, u32[]{:S(2)}) copy-start(bf16[2,48,1024]{2,1,0:T(8,128)(2,1)} %constant.7.clone.base_ref) | copy-start | bytes 589828
  0.0 53.5 %copy-start.1 = (f32[8,2,1024]{2,1,0:T(2,128)S(1)}, f32[8,2,1024]{2,1,0:T(2,128)}, u32[]{:S(2)}) copy-start(f32[8,2,1024]{2,1,0:T(2,128)} %constant.8.clone.turns_ref) | copy-start | bytes 196612

commit v8 on v5

--- a/solution.py
+++ b/solution.py
@@ -20,7 +20,7 @@
 PARTS = 8
 SLOTS = NFFT // 8 // PARTS
 USED = 4 * SLOTS
-CUTS = 4
+CUTS = 2
 LANES = 128
 WIDE = 2 * LANES
 

time: 79.6 us -> 79.6 us (level)
  no operation moved by 1% of the time
where the time goes in v8:
time: 79.6 us; the launch traced here: 78.4 us
  blocking collectives  69.6 us (87%)
  Pallas kernels  8.04 us (10%)
    all_to_all x3, blocking collectives, exchange(): return lax.all_to_all(value, axes, split_axis=0, concat_axis=0, tiled=True)  69.6 us
    pallas_call x1, Pallas kernels, bin_pairs(): pl.pallas_call(pairs_kernel, out_shape=jax.ShapeDtypeStruct((8, 48, WIDE)...  5.22 us
    pallas_call x1, Pallas kernels, make_spectra(): pl.pallas_call(spectra_kernel, out_shape=jax.ShapeDtypeStruct((4 * PARTS,...  2.18 us

profile of v8, /device:TPU:1, one launch (start us, length us, event | category | flops | bytes accessed | tf_op | source)
XLA Modules:
  0.0 78.4 jit_solution(8980312020065158488)
XLA Ops:
  0.0 0.0 copy-start.2
  0.0 0.0 copy-start
  0.0 0.0 copy-start.1
  0.0 2.2 %spectra.1 = bf16[32,16,256]{2,1,0:T(8,128)(2,1)S(1)} custom-call(bf16[16,768]{1,0:T(8,128)(2,1)} %bitcast.4, bf16[2,768,384]{2,1,0:T(8,128)(2,1)} %constant.8.clone.table_hbm, s32[2,512]{1,0:T(2,128)} %rows_hbm.1, s32[2,512]{1,0:T(2,128)} %bins_hbm.1, s32[1,512]{1,0:T(1,128)} %bitcast.5), custom_call_target="tpu_custom_call" | custom-call | tf_op jit(solution)/shard_map/spectra/pallas_call | solution.py:120
  2.2 32.5 %all_to_all.15 = bf16[32,16,256]{2,1,0:T(8,128)(2,1)S(1)} all-to-all(bf16[32,16,256]{2,1,0:T(8,128)(2,1)S(1)} %spectra.1), channel_id=1, replica_groups=mesh['x'=4,'zl'=8,'y'=4,'zh'=2,'core'=2] {'zl','x'}, dimensions={0} | all-to-all | bytes 524288 | tf_op jit(solution)/shard_map/all_to_all | solution.py:245
  34.7 0.0 copy-done.2
  34.7 5.2 %bin_pairs.1 = bf16[8,48,256]{2,1,0:T(8,128)(2,1)S(1)} custom-call(bf16[512,256]{1,0:T(8,128)(2,1)S(1)} %bitcast.3, s32[2,128]{1,0:T(2,128)S(1)} %copy-done.2), custom_call_target="tpu_custom_call" | custom-call | tf_op jit(solution)/shard_map/bin_pairs/pallas_call | solution.py:188
  39.9 13.6 %all_to_all.16.parts_ref = bf16[8,48,256]{2,1,0:T(8,128)(2,1)S(1)} all-to-all(bf16[8,48,256]{2,1,0:T(8,128)(2,1)S(1)} %bin_pairs.1), channel_id=1, replica_groups=mesh['x'=4,'zl'=8,'y'=4,'zh'=2,'core'=2] {'y','core'}, dimensions={0} | all-to-all | bytes 393216 | tf_op jit(solution)/shard_map/all_to_all | solution.py:245
  53.5 0.0 copy-done
  53.5 0.0 copy-done.1
  53.5 0.6 invert.1
  54.2 23.5 %all_to_all.17 = bf16[64,8,128]{2,1,0:T(8,128)(2,1)S(1)} all-to-all(bf16[64,8,128]{2,1,0:T(8,128)(2,1)S(1)} %invert.1), channel_id=1, replica_groups=mesh['x'=4,'zl'=8,'y'=4,'zh'=2,'core'=2] {'zh','zl','x'}, dimensions={0} | all-to-all | bytes 262144 | tf_op jit(solution)/shard_map/all_to_all | solution.py:245
  77.7 0.1 convert_reduce_fusion
  77.7 0.7 reshape.15
Async XLA Ops:
  0.0 34.7 %copy-start.2 = (s32[2,128]{1,0:T(2,128)S(1)}, s32[2,128]{1,0:T(2,128)}, u32[]{:S(2)}) copy-start(s32[2,128]{1,0:T(2,128)} %ids_ref.1) | copy-start | bytes 3076
  0.0 53.5 %copy-start = (bf16[2,48,1024]{2,1,0:T(8,128)(2,1)S(1)}, bf16[2,48,1024]{2,1,0:T(8,128)(2,1)}, u32[]{:S(2)}) copy-start(bf16[2,48,1024]{2,1,0:T(8,128)(2,1)} %constant.9.clone.base_ref) | copy-start | bytes 589828
  0.0 53.5 %copy-start.1 = (f32[8,2,1024]{2,1,0:T(2,128)S(1)}, f32[8,2,1024]{2,1,0:T(2,128)}, u32[]{:S(2)}) copy-start(f32[8,2,1024]{2,1,0:T(2,128)} %constant.10.clone.turns_ref) | copy-start | bytes 196612
